TPU v7x, 32 devices: a whole 2x2x4 slice. The times are simulated.
32 devices in a mesh: dp: 16 (over z, y, core), seq: 2 (over x).
Axes of the slice: x: 2, y: 2, z: 4, core: 2. Of those that a mesh axis runs over, the one named last changes fastest.
Arguments:
- tokens: bfloat16 [16384, 768], P(('dp', 'seq')), may hold values from -6 to 6
- w_qkv: bfloat16 [768, 2304], replicated, may hold values from -0.21875 to 0.21875
- w_out: bfloat16 [768, 768], replicated, may hold values from -0.875 to 0.875
- w_up: bfloat16 [768, 3072], replicated, may hold values from -0.21875 to 0.21875
- w_down: bfloat16 [3072, 768], replicated, may hold values from -0.109375 to 0.109375
- gains: float32 [2, 768], replicated, may hold values from 0.25 to 1.75
- biases: float32 [6, 768], replicated, may hold values from -2 to 2
- up_bias: float32 [3072], replicated, may hold values from -2 to 2
- image_cut: int32 [16], P('dp'), may hold values from 256 to 768, as said below
- group_live: int32 [16], P('dp'), may hold values from 768 to 1024, as said below
- cotangent: bfloat16 [16384, 768], P(('dp', 'seq')), may hold values from -6 to 6
Outputs:
- block_out: bfloat16 [16384, 768], P(('dp', 'seq'))
- grad_tokens: bfloat16 [16384, 768], P(('dp', 'seq'))
- grad_qkv: float32 [768, 2304], P(('dp', 'seq'))
- grad_wout: float32 [768, 768], P(('dp', 'seq'))
- grad_wup: float32 [768, 3072], P(('dp', 'seq'))
- grad_wdown: float32 [3072, 768], P(('dp', 'seq'))
- grad_gains: float32 [2, 768], P(None, ('dp', 'seq'))
- grad_biases: float32 [6, 768], P(None, ('dp', 'seq'))
- grad_upbias: float32 [3072], P(('dp', 'seq'))
Inputs may be any that keep to these rules, and one draw needn't show every extreme that they name: `group_live`: live rows of a group; the first group is full. The second image of a group spans rows image_cut to group_live - 1; each of a group's two images has 256 rows or more.
All inputs are finite; a program needn't handle non-finite values.
Results may differ from a plain program's by a relative error of at most 0.012.
Values may be sent and summed in bfloat16 or wider, within the bound.
No kernel may reach another device: no remote copies, remote signals or barrier semaphores. Data moves between devices by JAX's collectives and lax.ppermute only.
A program may use at most 192 MiB of HBM per device.

v0:
```python
from functools import partial

import jax
import jax.numpy as jnp
from jax import lax
from jax.sharding import PartitionSpec as P

HEADS = 12


EPSILON = 1e-06


def norm_rows(values, gain, shift):
    center = values - jnp.mean(values, axis=-1, keepdims=True)
    spread = jnp.mean(center * center, axis=-1, keepdims=True)
    return center * lax.rsqrt(spread + EPSILON) * gain + shift


def split_heads(values):
    return values.reshape(values.shape[0], HEADS, -1).transpose(1, 0, 2)


def join_heads(values):
    return values.transpose(1, 0, 2).reshape(values.shape[1], -1)


def head_probs(query_head, key_head, mask):
    raw = jnp.einsum("qd,kd->qk", query_head, key_head, preferred_element_type=jnp.float32)
    return jax.nn.softmax(raw * 0.125 + mask, axis=-1)


def shards(
    tokens, w_qkv, w_out, w_up, w_down, gains, biases, up_bias, image_cut, group_live, cotangent
):
    rows_here = tokens.shape[0]
    width = tokens.shape[1]
    group = rows_here * lax.axis_size("seq")
    first_row = lax.axis_index("seq") * rows_here
    cut_row = image_cut[0]
    live_rows = group_live[0]
    key_pos = jnp.arange(group, dtype=jnp.int32)
    query_pos = first_row + jnp.arange(rows_here, dtype=jnp.int32)
    query_live = (query_pos < live_rows)[:, None]
    allowed = ((query_pos >= cut_row)[:, None] == (key_pos >= cut_row)[None, :]) & (
        key_pos < live_rows
    )[None, :]
    mask = jnp.where(allowed, 0.0, -1000000000.0).astype(jnp.float32)
    inputs = tokens.astype(jnp.float32)
    normed_one, norm_back_one = jax.vjp(norm_rows, inputs, gains[0], biases[0])
    normed_one = normed_one.astype(jnp.bfloat16)
    projected = jnp.dot(normed_one, w_qkv, preferred_element_type=jnp.float32)
    queries = (projected[:, :width] + biases[2]).astype(jnp.bfloat16)
    key_rows = projected[:, width : 2 * width].astype(jnp.bfloat16)
    value_rows = (projected[:, 2 * width :] + biases[3]).astype(jnp.bfloat16)
    kv_local = jnp.concatenate([key_rows, value_rows], axis=1)
    kv_whole = lax.all_gather(kv_local, "seq", axis=0, tiled=True)
    query_heads = split_heads(queries)

    def attend(operands):
        query_head, key_head, value_head = operands
        probs = head_probs(query_head, key_head, mask)
        return jnp.dot(probs.astype(jnp.bfloat16), value_head, preferred_element_type=jnp.float32)

    heads_out = lax.map(
        attend, (query_heads, split_heads(kv_whole[:, :width]), split_heads(kv_whole[:, width:]))
    )
    attended = join_heads(heads_out).astype(jnp.bfloat16)
    residual = inputs + jnp.dot(attended, w_out, preferred_element_type=jnp.float32) + biases[4]
    normed_two, norm_back_two = jax.vjp(norm_rows, residual, gains[1], biases[1])
    normed_two = normed_two.astype(jnp.bfloat16)
    hidden_pre = jnp.dot(normed_two, w_up, preferred_element_type=jnp.float32) + up_bias
    activated, gelu_back = jax.vjp(partial(jax.nn.gelu, approximate=False), hidden_pre)
    activated = activated.astype(jnp.bfloat16)
    mlp_out = jnp.dot(activated, w_down, preferred_element_type=jnp.float32) + biases[5]
    block_out = jnp.where(query_live, residual + mlp_out, 0.0).astype(jnp.bfloat16)
    grad_live = jnp.where(query_live, cotangent, jnp.zeros_like(cotangent))
    grad_wdown = jnp.einsum("rf,rd->fd", activated, grad_live, preferred_element_type=jnp.float32)
    grad_activated = jnp.einsum("rd,fd->rf", grad_live, w_down, preferred_element_type=jnp.float32)
    grad_hidden = gelu_back(grad_activated)[0].astype(jnp.bfloat16)
    grad_wup = jnp.einsum("rd,rf->df", normed_two, grad_hidden, preferred_element_type=jnp.float32)
    grad_normed_two = jnp.einsum("rf,df->rd", grad_hidden, w_up, preferred_element_type=jnp.float32)
    grad_res_norm, gain_two, shift_two = norm_back_two(grad_normed_two)
    grad_residual = grad_live.astype(jnp.float32) + grad_res_norm
    grad_branch = grad_residual.astype(jnp.bfloat16)
    grad_wout = jnp.einsum("rd,re->de", attended, grad_branch, preferred_element_type=jnp.float32)
    grad_attended = jnp.einsum(
        "re,de->rd", grad_branch, w_out, preferred_element_type=jnp.float32
    ).astype(jnp.bfloat16)

    def attend_back(operands):
        query_head, key_head, value_head, grad_head = operands
        probs = head_probs(query_head, key_head, mask)
        grad_probs = jnp.einsum(
            "qd,kd->qk", grad_head, value_head, preferred_element_type=jnp.float32
        )
        grad_scores = probs * (grad_probs - jnp.sum(probs * grad_probs, axis=-1, keepdims=True))
        grad_raw = (grad_scores * 0.125).astype(jnp.bfloat16)
        grad_query = jnp.dot(grad_raw, key_head, preferred_element_type=jnp.float32)
        grad_key = jnp.einsum("qk,qd->kd", grad_raw, query_head, preferred_element_type=jnp.float32)
        grad_value = jnp.einsum(
            "qk,qd->kd", probs.astype(jnp.bfloat16), grad_head, preferred_element_type=jnp.float32
        )
        return (grad_query, grad_key, grad_value)

    grad_q_heads, grad_k_heads, grad_v_heads = lax.map(
        attend_back,
        (
            query_heads,
            split_heads(kv_whole[:, :width]),
            split_heads(kv_whole[:, width:]),
            split_heads(grad_attended),
        ),
    )
    grad_queries = join_heads(grad_q_heads).astype(jnp.bfloat16)
    grad_kv_terms = jnp.concatenate([join_heads(grad_k_heads), join_heads(grad_v_heads)], axis=1)
    grad_kv = lax.psum_scatter(
        grad_kv_terms.astype(jnp.bfloat16), "seq", scatter_dimension=0, tiled=True
    )
    grad_projected = jnp.concatenate([grad_queries, grad_kv], axis=1)
    grad_wqkv = jnp.einsum(
        "rd,re->de", normed_one, grad_projected, preferred_element_type=jnp.float32
    )
    grad_normed_one = jnp.einsum(
        "re,de->rd", grad_projected, w_qkv, preferred_element_type=jnp.float32
    )
    grad_in_norm, gain_one, shift_one = norm_back_one(grad_normed_one)
    grad_tokens = (grad_residual + grad_in_norm).astype(jnp.bfloat16)
    grad_gains = jnp.stack([gain_one, gain_two])
    grad_biases = jnp.stack(
        [
            shift_one,
            shift_two,
            jnp.sum(grad_queries.astype(jnp.float32), axis=0),
            jnp.sum(grad_kv[:, width:].astype(jnp.float32), axis=0),
            jnp.sum(grad_branch.astype(jnp.float32), axis=0),
            jnp.sum(grad_live.astype(jnp.float32), axis=0),
        ]
    )
    grad_upbias = jnp.sum(grad_hidden.astype(jnp.float32), axis=0)
    summed = (
        lax.psum_scatter(grad_wqkv, ("dp", "seq"), scatter_dimension=0, tiled=True),
        lax.psum_scatter(grad_wout, ("dp", "seq"), scatter_dimension=0, tiled=True),
        lax.psum_scatter(grad_wup, ("dp", "seq"), scatter_dimension=0, tiled=True),
        lax.psum_scatter(grad_wdown, ("dp", "seq"), scatter_dimension=0, tiled=True),
        lax.psum_scatter(grad_gains, ("dp", "seq"), scatter_dimension=1, tiled=True),
        lax.psum_scatter(grad_biases, ("dp", "seq"), scatter_dimension=1, tiled=True),
        lax.psum_scatter(grad_upbias, ("dp", "seq"), scatter_dimension=0, tiled=True),
    )
    return (
        block_out,
        grad_tokens,
        summed[0],
        summed[1],
        summed[2],
        summed[3],
        summed[4],
        summed[5],
        summed[6],
    )


def solution(mesh):
    in_specs = (
        P(("dp", "seq"), None),
        P(),
        P(),
        P(),
        P(),
        P(),
        P(),
        P(),
        P("dp"),
        P("dp"),
        P(("dp", "seq"), None),
    )
    out_specs = (
        P(("dp", "seq"), None),
        P(("dp", "seq"), None),
        P(("dp", "seq"), None),
        P(("dp", "seq"), None),
        P(("dp", "seq"), None),
        P(("dp", "seq"), None),
        P(None, ("dp", "seq")),
        P(None, ("dp", "seq")),
        P(("dp", "seq")),
    )
    return jax.shard_map(shards, mesh=mesh, in_specs=in_specs, out_specs=out_specs, check_vma=False)
```

profile of v0, /device:TPU:0, one launch (start us, length us, event | category | flops | bytes accessed | tf_op | source)
XLA Modules:
  0.0 882.6 jit_solution(543994483229277578)
XLA Ops:
  11.9 3.3 fusion.71
  18.1 2.3 copy.35
  20.4 2.5 copy.38
  25.4 40.3 %all-gather.2.cloned.1.call-done = bf16[1024,1536]{1,0:T(8,128)(2,1)} async-done(((bf16[512,1536]{1,0:T(8,128)(2,1)}), bf16[1024,1536]{1,0:T(8,128)(2,1)}) %all-gather.2.cloned.1.call-update) | async-done | bytes 3145744 | tf_op jit(solution)/shard_map/all_gather | solution.py:57
  65.7 3.8 fusion.84
  69.4 2.6 copy.36
  72.1 4.2 copy.39
  76.3 2.6 copy.37
  78.9 4.1 copy.40
  83.9 53.7 %while.26 = (s32[]{:T(128)}, bf16[12,512,64]{1,2,0:T(8,128)(2,1)}, bf16[12,512,64]{2,1,0:T(8,128)(2,1)}, bf16[12,1024,64]{2,1,0:T(8,128)(2,1)}, bf16[12,1024,64]...) while((s32[]{:T(128)}, bf16[12,512,64]{1,2,0:T(8,128)(2,1)}, ...), condition=%wide.region_5.6_spmd.clone, body=%wide.region_2.5_spmd.clone.sunk | while | flops 139983872 | bytes 7092829 | solution.py:65
  86.2 2.2 fusion.123
  95.2 2.2 fusion.123
  135.4 2.2 fusion.123
  138.2 2.8 fusion.85
  141.4 20.6 %multiply_convert_fusion.1 = (bf16[512,3072]{1,0:T(8,128)(2,1)}, f32[512,3072]{1,0:T(8,128)}, f32[512,3072]{1,0:T(8,128)}) fusion(f32[3072]{0:T(1024)} %param.22, bf16[768,3072]{1,0:T(8,128)(2,1)} %param.18, f32[512,768]{1,0:T(8,128)S(1)} %get-tuple-element.255, f32[768]{0:T(1024)S(1)} %copy-done.24, f32[768]{0:T(1024)S(1)} %get-tuple-element.262, ...), kind=kOutput, calls=%fused_computation.53 | convolution fusion | flops 2521694208 | bytes 22042624 | tf_op jit(solution)/shard_map/dot_general | solution.py:72
  162.1 9.3 %convert_reduce_fusion = (f32[3072]{0:T(1024)}, bf16[512,3072]{1,0:T(8,128)(2,1)}) fusion(f32[512,3072]{1,0:T(8,128)} %get-tuple-element.241, bf16[3072,768]{1,0:T(8,128)(2,1)S(1)} %bitcast.149, bf16[512,768]{1,0:T(8,128)(2,1)S(1)} %copy-done.5, pred[512]{0:T(512)(128)(4,1)S(1)} %get-tuple-element.264, f32[512,3072]{1,0:T(8,128)} %get-tuple-element.256, ...), kind=kOutput, calls=%fused_computation.51 | convolution fusion | flops 2443047936 | bytes 21258752 | tf_op jit(solution)/shard_map/rd,fd->rf/dot_general | solution.py:79
  171.4 5.5 multiply_reduce_fusion.1
  182.3 2.3 copy.41
  185.6 128.8 %while.27 = (s32[]{:T(128)}, bf16[12,512,64]{1,2,0:T(8,128)(2,1)}, bf16[12,1024,64]{1,2,0:T(8,128)(2,1)}, bf16[12,1024,64]{1,2,0:T(8,128)(2,1)}, bf16[12,512,64]...) while((s32[]{:T(128)}, bf16[12,512,64]{1,2,0:T(8,128)(2,1)}, ...), condition=%wide.region_14.15_spmd.clone, body=%wide.region_10.14_spmd.clone.sunk | while | flops 346552832 | bytes 19691124 | solution.py:106
  314.4 3.9 pad_maximum_fusion
  318.3 3.6 fusion.86
  322.0 9.0 %fusion.74 = f32[768,3072]{1,0:T(8,128)} fusion(bf16[512,3072]{1,0:T(8,128)(2,1)} %get-tuple-element.260, f32[512,768]{1,0:T(8,128)} %copy-done.4, f32[768]{0:T(1024)} %get-tuple-element.192, f32[768]{0:T(1024)S(1)} %get-tuple-element.262, f32[512]{0:T(512)S(1)} %fusion.67, f32[512]{0:T(512)S(1)} %broadcast_multiply_fusion), kind=kOutput, calls=%fused_computation.138 | convolution fusion | flops 2417885184 | bytes 14166016 | tf_op jit(solution)/shard_map/rd,rf->df/dot_general | solution.py:81
  331.3 8.4 fusion.76
  339.9 22.0 %reduce-scatter.8.cloned.1.call-done = bf16[512,1536]{0,1:T(8,128)(2,1)} async-done(((bf16[1024,1536]{0,1:T(8,128)(2,1)}), bf16[512,1536]{0,1:T(8,128)(2,1)}) %reduce-scatter.8.cloned.1.call-update) | async-done | bytes 1572880 | tf_op jit(solution)/shard_map/reduce_scatter | solution.py:117
  361.9 7.1 fusion.61
  374.2 7.5 select_convert_fusion
  381.7 3.5 fusion.78
  390.7 41.1 %all-reduce.3 = (f32[2,768]{1,0:T(2,128)S(1)}, f32[6,768]{1,0:T(8,128)}, f32[3072]{0:T(1024)}) all-reduce(f32[2,768]{1,0:T(2,128)S(1)} %pad_maximum_fusion.5, f32[6,768]{1,0:T(8,128)} %stack.27, f32[3072]{0:T(1024)} %get-tuple-element.259), channel_id=7, replica_groups=mesh['dp'=16,'seq'=2] {'dp','seq'}, use_global_device_ids=true, to_apply=%region_24.25.clone | all-reduce | flops 9216 | bytes 73728
  435.1 32.6 %reduce-scatter.12.cloned.1.call-done = f32[24,768]{1,0:T(8,128)} async-done(((f32[768,768]{1,0:T(8,128)}), f32[24,768]{1,0:T(8,128)}) %reduce-scatter.12.cloned.1.call-update) | async-done | bytes 73744 | tf_op jit(solution)/shard_map/reduce_scatter | solution.py:143
  467.6 141.5 %reduce-scatter.14.cloned.1.call-done = f32[24,3072]{1,0:T(8,128)} async-done(((f32[768,3072]{1,0:T(8,128)}), f32[24,3072]{1,0:T(8,128)}) %reduce-scatter.14.cloned.1.call-update) | async-done | bytes 294928 | tf_op jit(solution)/shard_map/reduce_scatter | solution.py:144
  609.1 141.5 %reduce-scatter.16.cloned.1.call-done = f32[96,768]{1,0:T(8,128)} async-done(((f32[3072,768]{1,0:T(8,128)}), f32[96,768]{1,0:T(8,128)}) %reduce-scatter.16.cloned.1.call-update) | async-done | bytes 294928 | tf_op jit(solution)/shard_map/reduce_scatter | solution.py:145
  750.7 124.6 %reduce-scatter.10.cloned.1.call-done = f32[24,2304]{1,0:T(8,128)} async-done(((f32[768,2304]{1,0:T(8,128)}), f32[24,2304]{1,0:T(8,128)}) %reduce-scatter.10.cloned.1.call-update) | async-done | bytes 221200 | tf_op jit(solution)/shard_map/reduce_scatter | solution.py:142
  (236 shorter events, 207.0 us)
Async XLA Ops:
  7.2 4.8 copy-start
  7.2 58.5 %all-gather.2.cloned.1.call-start = ((), (), s32[]{:S(2)}) async-start(), calls=%async_computation.5 | async-start | bytes 4718592 | tf_op jit(solution)/shard_map/all_gather | solution.py:57
  8.7 6.5 copy-start.11
  10.2 1.7 copy-start.18
  10.2 5.0 copy-start.13
  11.9 3.3 copy-start.9
  11.9 3.3 copy-start.22
  17.9 344.0 %reduce-scatter.8.cloned.1.call-start = ((), (), s32[]{:S(2)}) async-start(), calls=%async_computation.6 | async-start | bytes 4718592 | tf_op jit(solution)/shard_map/reduce_scatter | solution.py:117
  24.8 306.5 %copy-start.20 = (pred[512]{0:T(512)(128)(4,1)}, pred[512]{0:T(512)(128)(4,1)S(1)}, u32[]{:S(2)}) copy-start(pred[512]{0:T(512)(128)(4,1)S(1)} %get-tuple-element.264) | copy-start | bytes 1540
  138.2 3.1 copy-start.24
  138.2 23.8 %slice-start.2 = ((s8[4718592]{0:T(1024)(128)(4,1)}), s8[4194304]{0:T(1024)(128)(4,1)S(1)}, s32[]{:S(2)}) async-start(s8[4718592]{0:T(1024)(128)(4,1)} %bitcast.148), calls=%async_computation.13 | async-start | bytes 8388608
  138.2 33.2 %slice-start = ((s8[4718592]{0:T(1024)(128)(4,1)}), s8[4194304]{0:T(1024)(128)(4,1)S(1)}, s32[]{:S(2)}) async-start(s8[4718592]{0:T(1024)(128)(4,1)} %bitcast.146), calls=%async_computation.11 | async-start | bytes 8388608
  141.0 35.9 %copy-start.4 = (f32[512,768]{1,0:T(8,128)}, f32[512,768]{1,0:T(8,128)S(1)}, u32[]{:S(2)}) copy-start(f32[512,768]{1,0:T(8,128)S(1)} %get-tuple-element.255) | copy-start | bytes 4718596
  141.4 20.7 %copy-start.5 = (bf16[512,768]{1,0:T(8,128)(2,1)S(1)}, bf16[512,768]{1,0:T(8,128)(2,1)}, u32[]{:S(2)}) copy-start(bf16[512,768]{1,0:T(8,128)(2,1)} %param.25) | copy-start | bytes 2359300
  141.4 20.7 %slice-start.3 = ((s8[4718592]{0:T(1024)(128)(4,1)}), s8[524288]{0:T(1024)(128)(4,1)S(1)}, s32[]{:S(2)}) async-start(s8[4718592]{0:T(1024)(128)(4,1)} %bitcast.148), calls=%async_computation.14 | async-start | bytes 1048576
  141.4 20.7 %copy-start.27 = (f32[3072]{0:T(1024)S(1)}, f32[3072]{0:T(1024)}, u32[]{:S(2)}) copy-start(f32[3072]{0:T(1024)} %param.22) | copy-start | bytes 36868
  141.4 30.0 %slice-start.1 = ((s8[4718592]{0:T(1024)(128)(4,1)}), s8[524288]{0:T(1024)(128)(4,1)S(1)}, s32[]{:S(2)}) async-start(s8[4718592]{0:T(1024)(128)(4,1)} %bitcast.146), calls=%async_computation.12 | async-start | bytes 1048576
  177.6 3.1 copy-start.26
  177.6 2.1 copy-start.16
  318.3 149.3 %reduce-scatter.12.cloned.1.call-start = ((), (), s32[]{:S(2)}) async-start(), calls=%async_computation.8 | async-start | bytes 2433024 | tf_op jit(solution)/shard_map/reduce_scatter | solution.py:143
  322.0 287.2 %reduce-scatter.14.cloned.1.call-start = ((), (), s32[]{:S(2)}) async-start(), calls=%async_computation.9 | async-start | bytes 9732096 | tf_op jit(solution)/shard_map/reduce_scatter | solution.py:144
  331.0 419.7 %reduce-scatter.16.cloned.1.call-start = ((), (), s32[]{:S(2)}) async-start(), calls=%async_computation.10 | async-start | bytes 9732096 | tf_op jit(solution)/shard_map/reduce_scatter | solution.py:145
  339.8 22.1 %copy-start.10 = (f32[768]{0:T(1024)S(1)}, f32[768]{0:T(1024)}, u32[]{:S(2)}) copy-start(f32[768]{0:T(1024)} %copy-done.9) | copy-start | bytes 9220
  339.8 22.1 %copy-start.12 = (f32[512]{0:T(512)S(1)}, f32[512]{0:T(512)}, u32[]{:S(2)}) copy-start(f32[512]{0:T(512)} %copy-done.11) | copy-start | bytes 6148
  339.8 22.1 %copy-start.14 = (f32[512]{0:T(512)S(1)}, f32[512]{0:T(512)}, u32[]{:S(2)}) copy-start(f32[512]{0:T(512)} %copy-done.13) | copy-start | bytes 6148
  339.8 22.1 %copy-start.23 = (f32[768]{0:T(1024)S(1)}, f32[768]{0:T(1024)}, u32[]{:S(2)}) copy-start(f32[768]{0:T(1024)} %copy-done.22) | copy-start | bytes 9220
  339.8 535.5 %reduce-scatter.10.cloned.1.call-start = ((), (), s32[]{:S(2)}) async-start(), calls=%async_computation.7 | async-start | bytes 7299072 | tf_op jit(solution)/shard_map/reduce_scatter | solution.py:142
  374.2 7.5 copy-start.3
  374.2 7.5 copy-start.8
  381.7 3.5 copy-start.19
  381.7 3.5 copy-start.15
  385.2 1.6 copy-start.6
  (6 other events, 7.3 us)
Sparse Core Ops, SparseCore 0:
  18.0 47.6 all-gather.1
  318.4 43.4 reduce-scatter.7
  367.8 99.8 reduce-scatter.11
  473.9 135.1 reduce-scatter.13
  615.5 135.1 reduce-scatter.15
  756.8 118.4 reduce-scatter.9
where the time goes:
time: 889 us; the launch traced here: 883 us
  waiting for transfers between devices  503 us (57%)
  matrix products  245 us (28%)
  blocking collectives  41.1 us (5%)
  local copies, waits for them, and re-layouts  40.6 us (5%)
  other arithmetic  36.5 us (4%)
  between operations  16.2 us (2%)
    reduce_scatter x1, waiting for transfers between devices, shards(): lax.psum_scatter(grad_wup, ('dp', 'seq'), scatter_dimension=0, tiled=True)  142 us
    reduce_scatter x1, waiting for transfers between devices, shards(): lax.psum_scatter(grad_wdown, ('dp', 'seq'), scatter_dimension=0, tiled=True)  142 us
    reduce_scatter x1, waiting for transfers between devices, shards(): lax.psum_scatter(grad_wqkv, ('dp', 'seq'), scatter_dimension=0, tiled=True)  125 us
    dot_general x24, matrix products, head_probs(): jnp.einsum('qd,kd->qk', query_head, key_head, preferred_element_type=jnp....  41.9 us
    unnamed x1, blocking collectives  41.1 us
    all_gather x1, waiting for transfers between devices, shards(): kv_whole = lax.all_gather(kv_local, 'seq', axis=0, tiled=True)  40.3 us
    reduce_scatter x1, waiting for transfers between devices, shards(): lax.psum_scatter(grad_wout, ('dp', 'seq'), scatter_dimension=0, tiled=True)  32.6 us
    dot_general x12, matrix products, attend(): jnp.dot(probs.astype(jnp.bfloat16), value_head, preferred_element_type=jn...  26.6 us
  transfers between devices with their start and end apart: 6, of which 6 were waited for; matrix products, arithmetic and copies ran while one was open for 7% of the time, Pallas kernels for 0%

commit v1 on v0

--- a/solution.py
+++ b/solution.py
@@ -3,12 +3,715 @@
 import jax
 import jax.numpy as jnp
 from jax import lax
+from jax.experimental import pallas as pl
+from jax.experimental.pallas import tpu as pltpu
 from jax.sharding import PartitionSpec as P
 
 HEADS = 12
-
-
+HEAD_DIM = 64
+PAIR = 2 * HEAD_DIM
 EPSILON = 1e-06
+BOTH = ("dp", "seq")
+FAR = -1000000000.0
+F32 = jnp.float32
+BF16 = jnp.bfloat16
+
+ME, HALF, CUT, LIVE = 0, 1, 2, 3
+
+NN = (((1,), (0,)), ((), ()))
+NT = (((1,), (1,)), ((), ()))
+TN = (((0,), (0,)), ((), ()))
+
+
+def mm(a, b, dims=NN):
+    return lax.dot_general(a, b, dims, preferred_element_type=F32)
+
+
+def params(**more):
+    return pltpu.CompilerParams(vmem_limit_bytes=56 * 1024 * 1024, **more)
+
+
+def norm_parts(values):
+    center = values - jnp.mean(values, axis=-1, keepdims=True)
+    spread = jnp.mean(center * center, axis=-1, keepdims=True)
+    rstd = lax.rsqrt(spread + EPSILON)
+    return center * rstd, rstd
+
+
+def norm_back(grad, unit, rstd, gain):
+    scaled = grad * gain
+    first = jnp.mean(scaled, axis=-1, keepdims=True)
+    second = jnp.mean(scaled * unit, axis=-1, keepdims=True)
+    return rstd * (scaled - first - unit * second)
+
+
+def hop(value, mask, count):
+    return lax.ppermute(value, BOTH, [(i, i ^ mask) for i in range(count)])
+
+
+def add_up(a, b):
+    return a.astype(F32) + b.astype(F32)
+
+
+def reduce_streams(streams, count):
+    state = [(keep, send) for keep, send, _ in streams]
+    depth = len(streams[0][2])
+    for step in range(depth):
+        got = [hop(send, masks[step], count) for (_, send), (_, _, masks) in zip(state, streams)]
+        following = []
+        for (keep, _), arrived in zip(state, got):
+            if step + 1 < depth:
+                send = add_up(keep[1], arrived[1]).astype(BF16)
+                keep = add_up(keep[0], arrived[0]).astype(BF16)
+                following.append((keep, send))
+            else:
+                following.append((add_up(keep, arrived), None))
+        state = following
+    return [keep for keep, _ in state]
+
+
+def places(masks):
+    out = [((), 0)]
+    for mask in masks:
+        out = [(at + (bit,), value ^ (mask * bit)) for at, value in out for bit in (0, 1)]
+    return out
+
+
+def qkv_kernel(meta, mine, other, wq, wk, wv, gains, biases, n1_ref, q_ref, k_ref, v_ref):
+    step = pl.program_id(0)
+
+    def run(ref):
+        unit, _ = norm_parts(ref[...].astype(F32))
+        normed = (unit * gains[0:1, :] + biases[0:1, :]).astype(BF16)
+        n1_ref[...] = normed
+        half = q_ref.shape[1]
+        first = pl.multiple_of(meta[HALF] * half, half)
+        q_ref[...] = (mm(normed, wq[...]) + biases_at(biases, 2, first, half)).astype(BF16)
+        k_ref[...] = mm(normed, wk[...]).astype(BF16)
+        v_ref[...] = (mm(normed, wv[...]) + biases_at(biases, 3, first, half)).astype(BF16)
+
+    @pl.when(step == 0)
+    def _():
+        run(mine)
+
+    @pl.when(step == 1)
+    def _():
+        run(other)
+
+
+def biases_at(biases, row, first, size):
+    return biases[row : row + 1, pl.ds(first, size)]
+
+
+def qkv_call(meta, mine, other, w_qkv, gains, biases):
+    rows, width = mine.shape
+    half = width // 2
+    full = lambda shape: pl.BlockSpec(shape, lambda i, m: (0, 0))
+    weight = lambda part: pl.BlockSpec((width, half), lambda i, m: (0, 2 * part + m[HALF]))
+    out = lambda cols: pl.BlockSpec((rows, cols), lambda i, m: (i ^ m[HALF], 0))
+    shape = lambda cols: jax.ShapeDtypeStruct((2 * rows, cols), BF16)
+    return pl.pallas_call(
+        qkv_kernel,
+        grid_spec=pltpu.PrefetchScalarGridSpec(
+            num_scalar_prefetch=1,
+            grid=(2,),
+            in_specs=[
+                full((rows, width)), full((rows, width)), weight(0), weight(1), weight(2),
+                full(gains.shape), full(biases.shape),
+            ],
+            out_specs=[out(width), out(half), out(half), out(half)],
+        ),
+        out_shape=[shape(width), shape(half), shape(half), shape(half)],
+        compiler_params=params(),
+        name="qkv",
+    )(meta, mine, other, w_qkv, w_qkv, w_qkv, gains, biases)
+
+
+TILE = 256
+
+
+def lanes(rows):
+    return lax.broadcasted_iota(jnp.int32, (rows, PAIR), 1)
+
+
+def own_lanes(rows, head):
+    return (lanes(rows) // HEAD_DIM) == head
+
+
+def key_side(key_pair, head, meta):
+    rows = key_pair.shape[0]
+    at = lanes(rows) - (1 - head) * HEAD_DIM
+    pos = lax.broadcasted_iota(jnp.int32, (rows, PAIR), 0)
+    alive = pos < meta[LIVE]
+    second = pos >= meta[CUT]
+    in_first = alive & jnp.logical_not(second)
+    in_second = alive & second
+    extra = jnp.where(
+        ((at == 0) & jnp.logical_not(in_first)) | ((at == 1) & jnp.logical_not(in_second)), FAR, 0.0
+    )
+    return jnp.where(own_lanes(rows, head), key_pair.astype(F32), extra).astype(BF16)
+
+
+def query_side(query_pair, head, first_row, meta):
+    rows = query_pair.shape[0]
+    at = lanes(rows) - (1 - head) * HEAD_DIM
+    second = first_row + lax.broadcasted_iota(jnp.int32, (rows, PAIR), 0) >= meta[CUT]
+    extra = jnp.where(
+        ((at == 0) & jnp.logical_not(second)) | ((at == 1) & second), 1.0, 0.0
+    )
+    return jnp.where(own_lanes(rows, head), query_pair.astype(F32) * 0.125, extra).astype(BF16)
+
+
+def key_range(first_row, group, meta):
+    cut = meta[CUT]
+    live = meta[LIVE]
+    only_first = first_row + TILE <= cut
+    only_second = first_row >= cut
+    low = jnp.where(only_second, cut, 0)
+    high = jnp.where(only_first, cut, live)
+    low = (low // 128) * 128
+    steps = (high - low + (TILE - 1)) // TILE
+    start = jnp.minimum(low, group - steps * TILE)
+    return pl.multiple_of(start, 128), steps
+
+
+def by_width(steps, group, body):
+    for count in range(1, group // TILE + 1):
+
+        @pl.when(steps == count)
+        def _(count=count):
+            body(count * TILE)
+
+
+def attend_kernel(meta, which, q_ref, k_ref, v_ref, o_ref, lse_ref, kx_ref, vt_ref):
+    rows = q_ref.shape[0]
+    group = k_ref.shape[0]
+    base = which[0] * rows
+    for head in (0, 1):
+        kx_ref[head] = key_side(k_ref[...], head, meta)
+    vt_ref[...] = v_ref[...].T
+
+    def tile(index, carry):
+        at = pl.multiple_of(index * TILE, TILE)
+        first_row = base + at
+        start, steps = key_range(first_row, group, meta)
+        query = q_ref[pl.ds(at, TILE), :]
+
+        def body(width):
+            parts = []
+            for head in (0, 1):
+                qx = query_side(query, head, first_row, meta)
+                scores = mm(kx_ref[head, pl.ds(start, width), :], qx, NT)
+                top = jnp.max(scores, axis=0, keepdims=True)
+                weight = jnp.exp(scores - top).astype(BF16)
+                value = vt_ref[head * HEAD_DIM : (head + 1) * HEAD_DIM, pl.ds(start, width)]
+                left = jnp.concatenate([value, jnp.ones((16, width), BF16)], axis=0)
+                both = mm(left, weight)
+                total = both[HEAD_DIM : HEAD_DIM + 1, :]
+                parts.append(both[:HEAD_DIM, :] / total)
+                lse_ref[0, head : head + 1, pl.ds(at, TILE)] = top + jnp.log(total)
+            o_ref[pl.ds(at, TILE), :] = jnp.concatenate(parts, axis=0).T.astype(BF16)
+
+        by_width(steps, group, body)
+        return carry
+
+    lax.fori_loop(0, rows // TILE, tile, 0)
+
+
+def attend_call(meta, which, q, k, v):
+    group, half = q.shape
+    rows = group // 2
+    pairs = half // PAIR
+    return pl.pallas_call(
+        attend_kernel,
+        grid_spec=pltpu.PrefetchScalarGridSpec(
+            num_scalar_prefetch=2,
+            grid=(pairs,),
+            in_specs=[
+                pl.BlockSpec((rows, PAIR), lambda p, m, w: (w[0], p)),
+                pl.BlockSpec((group, PAIR), lambda p, m, w: (0, p)),
+                pl.BlockSpec((group, PAIR), lambda p, m, w: (0, p)),
+            ],
+            out_specs=[
+                pl.BlockSpec((rows, PAIR), lambda p, m, w: (0, p)),
+                pl.BlockSpec((1, 2, rows), lambda p, m, w: (p, 0, 0)),
+            ],
+            scratch_shapes=[pltpu.VMEM((2, group, PAIR), BF16), pltpu.VMEM((PAIR, group), BF16)],
+        ),
+        out_shape=[
+            jax.ShapeDtypeStruct((rows, half), BF16),
+            jax.ShapeDtypeStruct((pairs, 2, rows), F32),
+        ],
+        compiler_params=params(),
+        name="attend",
+    )(meta, which, q, k, v)
+
+
+def attend_back_kernel(
+    meta, q_ref, k_ref, v_ref, do_mine, do_other, o_mine, o_other, lse_mine, lse_other,
+    dq_ref, dk_ref, dv_ref, kx_ref, kt_ref, dk_acc, dv_acc,
+):
+    group = k_ref.shape[0]
+    rows = do_mine.shape[0]
+    for head in (0, 1):
+        kx_ref[head] = key_side(k_ref[...], head, meta)
+    kt_ref[...] = k_ref[...].T
+    dk_acc[...] = jnp.zeros_like(dk_acc)
+    dv_acc[...] = jnp.zeros_like(dv_acc)
+    for place, do_ref, o_ref, lse_ref in (
+        (0, do_mine, o_mine, lse_mine), (1, do_other, o_other, lse_other),
+    ):
+        base = (meta[HALF] ^ place) * rows
+
+        def tile(index, carry, do_ref=do_ref, o_ref=o_ref, lse_ref=lse_ref, base=base):
+            at = pl.multiple_of(index * TILE, TILE)
+            first_row = pl.multiple_of(base + at, TILE)
+            start, steps = key_range(first_row, group, meta)
+            query = q_ref[pl.ds(first_row, TILE), :]
+            grad = do_ref[pl.ds(at, TILE), :]
+            dots = (grad.astype(F32) * o_ref[pl.ds(at, TILE), :].astype(F32)).T
+
+            def body(width):
+                probs, raws, masked_grads, masked_queries, dqs = [], [], [], [], []
+                for head in (0, 1):
+                    mine = own_lanes(TILE, head)
+                    qx = query_side(query, head, first_row, meta)
+                    dox = jnp.where(mine, grad, jnp.zeros_like(grad))
+                    scores = mm(kx_ref[head, pl.ds(start, width), :], qx, NT)
+                    prob = jnp.exp(scores - lse_ref[0, head : head + 1, pl.ds(at, TILE)])
+                    gprob = mm(v_ref[pl.ds(start, width), :], dox, NT)
+                    delta = jnp.sum(dots[head * HEAD_DIM : (head + 1) * HEAD_DIM, :], axis=0, keepdims=True)
+                    raw = (prob * (gprob - delta)).astype(BF16)
+                    keys_t = kt_ref[head * HEAD_DIM : (head + 1) * HEAD_DIM, pl.ds(start, width)]
+                    dqs.append(mm(keys_t, raw))
+                    probs.append(prob.astype(BF16))
+                    raws.append(raw)
+                    masked_grads.append(dox)
+                    masked_queries.append(jnp.where(mine, query * jnp.asarray(0.125, BF16), jnp.zeros_like(query)))
+                dv_acc[pl.ds(start, width), :] += mm(
+                    jnp.concatenate(probs, axis=1), jnp.concatenate(masked_grads, axis=0)
+                )
+                dk_acc[pl.ds(start, width), :] += mm(
+                    jnp.concatenate(raws, axis=1), jnp.concatenate(masked_queries, axis=0)
+                )
+                dq = jnp.concatenate(dqs, axis=0).T * 0.125
+                dq_ref[pl.ds(first_row, TILE), :] = dq.astype(BF16)
+
+            by_width(steps, group, body)
+            return carry
+
+        lax.fori_loop(0, rows // TILE, tile, 0)
+    dk_ref[...] = dk_acc[...].astype(BF16)
+    dv_ref[...] = dv_acc[...].astype(BF16)
+
+
+def attend_back_call(meta, q, k, v, do_mine, do_other, o_mine, o_other, lse_mine, lse_other, first, count):
+    group, half = q.shape
+    rows = group // 2
+    whole = pl.BlockSpec((group, PAIR), lambda p, m: (0, p + first))
+    part = pl.BlockSpec((rows, PAIR), lambda p, m: (0, p + first))
+    lse = pl.BlockSpec((1, 2, rows), lambda p, m: (p + first, 0, 0))
+    out = pl.BlockSpec((group, PAIR), lambda p, m: (0, p))
+    return pl.pallas_call(
+        attend_back_kernel,
+        grid_spec=pltpu.PrefetchScalarGridSpec(
+            num_scalar_prefetch=1,
+            grid=(count,),
+            in_specs=[whole, whole, whole, part, part, part, part, lse, lse],
+            out_specs=[out, out, out],
+            scratch_shapes=[
+                pltpu.VMEM((2, group, PAIR), BF16),
+                pltpu.VMEM((PAIR, group), BF16),
+                pltpu.VMEM((group, PAIR), F32),
+                pltpu.VMEM((group, PAIR), F32),
+            ],
+        ),
+        out_shape=[jax.ShapeDtypeStruct((group, count * PAIR), BF16)] * 3,
+        compiler_params=params(),
+        name="attend_back",
+    )(meta, q, k, v, do_mine, do_other, o_mine, o_other, lse_mine, lse_other)
+
+
+CORE, SIDE_X, SIDE_Y, Z_NEAR, Z_FAR = 2, 1, 4, 8, 24
+ORDER_ZXY = (CORE, Z_NEAR, Z_FAR, SIDE_X, SIDE_Y)
+ORDER_XYZ = (CORE, SIDE_X, SIDE_Y, Z_NEAR, Z_FAR)
+ORDER_YXZ = (CORE, SIDE_Y, SIDE_X, Z_NEAR, Z_FAR)
+ORDERS = (ORDER_ZXY, ORDER_XYZ, ORDER_YXZ)
+COUNT = 32
+UP_STEPS = ((0, 2), (2, 5), (5, 8))
+DOWN_ROWS = ((0, 24), (24, 64), (64, 96))
+OUT_COLS = ((0, 128), (128, 512), (512, 768))
+
+ERF_TOP = (0.00022905065861350646, 0.0034082910107109506, 0.050955695062380861, 0.18520832239976145, 1.128379143519084)
+ERF_LOW = (
+    -1.1791602954361697e-7, 0.000023547966471313185, 0.0010179625278914885, 0.014070470171167667,
+    0.11098505178285362, 0.49746925110067538, 1.0,
+)
+
+
+def erf(x):
+    x = jnp.clip(x, -3.832506856900711, 3.832506856900711)
+    square = x * x
+    top = jnp.full_like(x, ERF_TOP[0])
+    for c in ERF_TOP[1:]:
+        top = top * square + c
+    low = jnp.full_like(x, ERF_LOW[0])
+    for c in ERF_LOW[1:]:
+        low = low * square + c
+    return x * top / low
+
+
+def put_parts(source, me, masks, keep, send, rows, here=lambda at: at):
+    for bit, ref in ((0, keep), (1, send)):
+        for at, value in places(masks[1:]):
+            target = me ^ (value ^ (masks[0] * bit))
+            first = pl.multiple_of(target * rows, 8)
+            ref[here(at)] = source[pl.ds(first, rows), :].astype(BF16)
+
+
+def mid_kernel(
+    meta, tok, cot, a_own, a_got, w_out, w_up, w_down, gains, biases, up_bias,
+    block_ref, gres_ref, gb_ref, ga_own, ga_send, small_ref, gub_ref,
+    up0k, up0s, up1k, up1s, up2k, up2s, dn0k, dn0s, dn1k, dn1s, dn2k, dn2s,
+    res_ref, n2_ref, n2t_ref, gl_ref, out_acc, dn_acc, up_blk, down_blk,
+):
+    step = pl.program_id(0)
+    rows, width = tok.shape
+    half = a_own.shape[1]
+    me = meta[ME]
+    own = pl.multiple_of(meta[HALF] * half, half)
+    far = pl.multiple_of((1 - meta[HALF]) * half, half)
+    live = meta[HALF] * rows + lax.broadcasted_iota(jnp.int32, (rows, 1), 0) < meta[LIVE]
+
+    @pl.when(step == 0)
+    def _():
+        residual = (
+            tok[...].astype(F32)
+            + mm(a_own[...], w_out[pl.ds(own, half), :])
+            + mm(a_got[...], w_out[pl.ds(far, half), :])
+            + biases[4:5, :]
+        )
+        res_ref[...] = residual
+        unit, _ = norm_parts(residual)
+        n2 = (unit * gains[1:2, :] + biases[1:2, :]).astype(BF16)
+        n2_ref[...] = n2
+        n2t_ref[...] = n2.T
+        gl_ref[...] = jnp.where(live, cot[...], jnp.zeros_like(cot))
+        out_acc[...] = jnp.zeros_like(out_acc)
+        dn_acc[...] = jnp.zeros_like(dn_acc)
+
+    hidden = mm(n2_ref[...], w_up[...]) + up_bias[...]
+    gact = mm(gl_ref[...], w_down[...], NT)
+    cdf = 0.5 * (1.0 + erf(hidden * 0.7071067811865476))
+    pdf = jnp.exp(-0.5 * hidden * hidden) * 0.3989422804014327
+    act = (hidden * cdf).astype(BF16)
+    grad_hidden = gact * (cdf + hidden * pdf)
+    gub_ref[...] = jnp.sum(grad_hidden, axis=0, keepdims=True)
+    grad_hidden = grad_hidden.astype(BF16)
+    out_acc[...] += mm(act, w_down[...])
+    dn_acc[...] += mm(grad_hidden, w_up[...], NT)
+    down_blk[...] = mm(act, gl_ref[...], TN)
+    up_blk[...] = mm(n2t_ref[...], grad_hidden)
+
+    part = down_blk.shape[0] // 4
+    for (low, high), masks, keep, send in zip(DOWN_ROWS, ORDERS, (dn0k, dn1k, dn2k), (dn0s, dn1s, dn2s)):
+        dim = masks.index(SIDE_X) - 1
+        for bit, ref in ((0, keep), (1, send)):
+            for x_bit in (0, 1):
+                target = (me & 3) ^ (bit * CORE + x_bit * SIDE_X)
+                at = tuple(x_bit if i == dim else 0 for i in range(4))
+                first = pl.multiple_of(target * part + low, 8)
+                ref[at] = down_blk[pl.ds(first, high - low), :].astype(BF16)
+
+    for (low, high), masks, keep, send in zip(UP_STEPS, ORDERS, (up0k, up1k, up2k), (up0s, up1s, up2s)):
+
+        @pl.when((step >= low) & (step < high))
+        def _(masks=masks, keep=keep, send=send):
+            put_parts(up_blk, me, masks, keep, send, width // COUNT)
+
+    @pl.when(step == pl.num_programs(0) - 1)
+    def _():
+        residual = res_ref[...]
+        block_ref[...] = jnp.where(live, residual + out_acc[...] + biases[5:6, :], 0.0).astype(BF16)
+        unit, rstd = norm_parts(residual)
+        grad = dn_acc[...]
+        gl = gl_ref[...].astype(F32)
+        gres = gl + norm_back(grad, unit, rstd, gains[1:2, :])
+        gb = gres.astype(BF16)
+        gres_ref[...] = gres
+        gb_ref[...] = gb
+        ga_send[...] = mm(gb, w_out[pl.ds(far, half), :], NT).astype(BF16)
+        ga_own[...] = mm(gb, w_out[pl.ds(own, half), :], NT).astype(BF16)
+        small_ref[0:1, :] = jnp.sum(grad * unit, axis=0, keepdims=True)
+        small_ref[1:2, :] = jnp.sum(grad, axis=0, keepdims=True)
+        small_ref[2:3, :] = jnp.sum(gb.astype(F32), axis=0, keepdims=True)
+        small_ref[3:4, :] = jnp.sum(gl, axis=0, keepdims=True)
+        small_ref[4:8, :] = jnp.zeros((4, width), F32)
+
+
+def mid_call(meta, tok, cot, a_own, a_got, w_out, w_up, w_down, gains, biases, up_bias):
+    rows, width = tok.shape
+    ff = w_up.shape[1]
+    steps = COUNT // 4
+    chunk = ff // steps
+    part = width // COUNT
+
+    def full(shape):
+        return pl.BlockSpec(shape, lambda i, m: (0,) * len(shape))
+
+    def up_spec(low, high):
+        return pl.BlockSpec(
+            (2, 2, 2, 2, part, chunk),
+            lambda i, m: (0, 0, 0, 0, 0, jnp.clip(i - low, 0, high - low - 1)),
+        )
+
+    def down_spec(masks, size):
+        def at(i, m):
+            column = i ^ (m[ME] // 4)
+            z = column // 2
+            bits = {SIDE_Y: column % 2, Z_FAR: z // 2, Z_NEAR: (z % 2) ^ (z // 2), SIDE_X: 0}
+            return tuple(bits[mask] for mask in masks[1:]) + (0, 0)
+
+        return pl.BlockSpec(tuple(2 if mask == SIDE_X else 1 for mask in masks[1:]) + (size, width), at)
+
+    out_specs = [
+        full((rows, width)), full((rows, width)), full((rows, width)),
+        full((rows, width // 2)), full((rows, width // 2)), full((8, width)),
+        pl.BlockSpec((1, chunk), lambda i, m: (0, i)),
+    ]
+    out_shape = [
+        jax.ShapeDtypeStruct((rows, width), BF16), jax.ShapeDtypeStruct((rows, width), F32),
+        jax.ShapeDtypeStruct((rows, width), BF16), jax.ShapeDtypeStruct((rows, width // 2), BF16),
+        jax.ShapeDtypeStruct((rows, width // 2), BF16), jax.ShapeDtypeStruct((8, width), F32),
+        jax.ShapeDtypeStruct((1, ff), F32),
+    ]
+    for low, high in UP_STEPS:
+        out_specs += [up_spec(low, high)] * 2
+        out_shape += [jax.ShapeDtypeStruct((2, 2, 2, 2, part, (high - low) * chunk), BF16)] * 2
+    for (low, high), masks in zip(DOWN_ROWS, ORDERS):
+        out_specs += [down_spec(masks, high - low)] * 2
+        out_shape += [jax.ShapeDtypeStruct((2, 2, 2, 2, high - low, width), BF16)] * 2
+    out = pl.pallas_call(
+        mid_kernel,
+        grid_spec=pltpu.PrefetchScalarGridSpec(
+            num_scalar_prefetch=1,
+            grid=(steps,),
+            in_specs=[
+                full((rows, width)), full((rows, width)), full((rows, width // 2)), full((rows, width // 2)),
+                full(w_out.shape),
+                pl.BlockSpec((width, chunk), lambda i, m: (0, i)),
+                pl.BlockSpec((chunk, width), lambda i, m: (i, 0)),
+                full(gains.shape), full(biases.shape),
+                pl.BlockSpec((1, chunk), lambda i, m: (0, i)),
+            ],
+            out_specs=out_specs,
+            scratch_shapes=[
+                pltpu.VMEM((rows, width), F32), pltpu.VMEM((rows, width), BF16), pltpu.VMEM((width, rows), BF16),
+                pltpu.VMEM((rows, width), BF16), pltpu.VMEM((rows, width), F32), pltpu.VMEM((rows, width), F32),
+                pltpu.VMEM((width, chunk), F32), pltpu.VMEM((chunk, width), F32),
+            ],
+        ),
+        out_shape=out_shape,
+        compiler_params=params(),
+        name="mid",
+    )(meta, tok, cot, a_own, a_got, w_out, w_up, w_down, gains, biases, up_bias.reshape(1, ff))
+    up = [(out[7 + 2 * i], out[8 + 2 * i], ORDERS[i]) for i in range(3)]
+    down = [(out[13 + 2 * i], out[14 + 2 * i], ORDERS[i]) for i in range(3)]
+    return out[:7], up, down
+
+
+def wout_kernel(meta, a_own, a_got, gb, k0, s0, k1, s1, k2, s2, whole):
+    half = a_own.shape[1]
+    own = pl.multiple_of(meta[HALF] * half, half)
+    far = pl.multiple_of((1 - meta[HALF]) * half, half)
+    whole[pl.ds(own, half), :] = mm(a_own[...], gb[...], TN)
+    whole[pl.ds(far, half), :] = mm(a_got[...], gb[...], TN)
+    part = whole.shape[0] // COUNT
+    for (low, high), masks, keep, send in zip(OUT_COLS, ORDERS, (k0, k1, k2), (s0, s1, s2)):
+        put_parts(whole.at[:, low:high], meta[ME], masks, keep, send, part)
+
+
+def wout_call(meta, a_own, a_got, gb):
+    rows, width = gb.shape
+    out_shape = []
+    for low, high in OUT_COLS:
+        out_shape += [jax.ShapeDtypeStruct((2, 2, 2, 2, width // COUNT, high - low), BF16)] * 2
+    out = pl.pallas_call(
+        wout_kernel,
+        grid_spec=pltpu.PrefetchScalarGridSpec(
+            num_scalar_prefetch=1,
+            grid=(1,),
+            in_specs=[pl.BlockSpec(a.shape, lambda i, m: (0, 0)) for a in (a_own, a_got, gb)],
+            out_specs=[pl.BlockSpec(s.shape, lambda i, m: (0,) * 6) for s in out_shape],
+            scratch_shapes=[pltpu.VMEM((width, width), F32)],
+        ),
+        out_shape=out_shape,
+        compiler_params=params(),
+        name="wout",
+    )(meta, a_own, a_got, gb)
+    return [(out[2 * i], out[2 * i + 1], ORDERS[i]) for i in range(3)]
+
+
+QKV_ORDERS = (
+    (SIDE_X, SIDE_Y, Z_NEAR, Z_FAR, CORE), (SIDE_Y, SIDE_X, Z_NEAR, Z_FAR, CORE), (Z_NEAR, Z_FAR, SIDE_Y, SIDE_X, CORE),
+)
+SMALL = 128
+
+
+def qkv_back_kernel(
+    meta, n1, dq, dk, dv, wq, wk, wv, tok_mine, tok_other, early,
+    dn_own, dn_send, qk, qs, kk, ks, vk, vs, n1t, dn_acc, block, late,
+):
+    me = meta[ME]
+    rows, width = tok_mine.shape
+    half = dq.shape[1]
+    part = width // COUNT
+    own = pl.multiple_of(meta[HALF] * half, half)
+    n1t[...] = n1[...].T
+    late[...] = jnp.zeros_like(late)
+    late[4:5, pl.ds(own, half)] = jnp.sum(dq[...].astype(F32), axis=0, keepdims=True)
+    late[5:6, pl.ds(own, half)] = jnp.sum(dv[...].astype(F32), axis=0, keepdims=True)
+    dn_acc[...] = mm(dq[...], wq[...], NT) + mm(dk[...], wk[...], NT) + mm(dv[...], wv[...], NT)
+    mine = pl.multiple_of(meta[HALF] * rows, rows)
+    other = pl.multiple_of((1 - meta[HALF]) * rows, rows)
+    dn_send[...] = dn_acc[pl.ds(other, rows), :].astype(BF16)
+    dn_own[...] = dn_acc[pl.ds(mine, rows), :]
+    gain = jnp.zeros((1, width), F32)
+    for place, tok in ((mine, tok_mine), (other, tok_other)):
+        unit, _ = norm_parts(tok[...].astype(F32))
+        gain += jnp.sum(dn_acc[pl.ds(place, rows), :] * unit, axis=0, keepdims=True)
+    late[0:1, :] = gain
+    late[2:3, :] = jnp.sum(dn_acc[...], axis=0, keepdims=True)
+    for grad, masks, keep, send in zip((dq, dk, dv), QKV_ORDERS, (qk, kk, vk), (qs, ks, vs)):
+        block[:, :half] = mm(n1t[...], grad[...])
+        cols = half
+        if grad is dv:
+            cols = half + SMALL
+            block[:, half:] = late[...].T + early[...]
+        put_parts(block.at[:, :cols], me, masks, keep, send, part)
+
+
+def qkv_back_call(meta, n1, dq, dk, dv, w_qkv, tok_mine, tok_other, early):
+    group, width = n1.shape
+    half = dq.shape[1]
+    part = width // COUNT
+
+    def full(shape):
+        return pl.BlockSpec(shape, lambda i, m: (0,) * len(shape))
+
+    def weight(which):
+        return pl.BlockSpec((width, half), lambda i, m: (0, 2 * which + m[HALF]))
+
+    rows = group // 2
+    out_shape = [jax.ShapeDtypeStruct((rows, width), F32), jax.ShapeDtypeStruct((rows, width), BF16)]
+    for cols in (half, half, half + SMALL):
+        out_shape += [jax.ShapeDtypeStruct((2, 2, 2, 2, part, cols), BF16)] * 2
+    out = pl.pallas_call(
+        qkv_back_kernel,
+        grid_spec=pltpu.PrefetchScalarGridSpec(
+            num_scalar_prefetch=1,
+            grid=(1,),
+            in_specs=[
+                full(n1.shape), full(dq.shape), full(dk.shape), full(dv.shape), weight(0), weight(1), weight(2),
+                full(tok_mine.shape), full(tok_other.shape), full(early.shape),
+            ],
+            out_specs=[full(s.shape) for s in out_shape],
+            scratch_shapes=[
+                pltpu.VMEM((width, group), BF16), pltpu.VMEM((group, width), F32),
+                pltpu.VMEM((width, half + SMALL), F32), pltpu.VMEM((SMALL, width), F32),
+            ],
+        ),
+        out_shape=out_shape,
+        compiler_params=params(),
+        name="qkv_back",
+    )(meta, n1, dq, dk, dv, w_qkv, w_qkv, w_qkv, tok_mine, tok_other, early)
+    streams = [(out[2 + 2 * i], out[3 + 2 * i], QKV_ORDERS[i][:-1]) for i in range(3)]
+    return out[0], out[1], streams
+
+
+def tail_kernel(tok, gres, dn_own, dn_got, gains, out):
+    unit, rstd = norm_parts(tok[...].astype(F32))
+    grad = dn_own[...] + dn_got[...].astype(F32)
+    out[...] = (gres[...] + norm_back(grad, unit, rstd, gains[0:1, :])).astype(BF16)
+
+
+def tail_call(tok, gres, dn_own, dn_got, gains):
+    rows, width = tok.shape
+    block = pl.BlockSpec((rows // 4, width), lambda i: (i, 0))
+    return pl.pallas_call(
+        tail_kernel,
+        grid=(4,),
+        in_specs=[block, block, block, block, pl.BlockSpec(gains.shape, lambda i: (0, 0))],
+        out_specs=block,
+        out_shape=jax.ShapeDtypeStruct((rows, width), BF16),
+        compiler_params=params(),
+        name="tail",
+    )(tok, gres, dn_own, dn_got, gains)
+
+
+def paired(
+    tokens, w_qkv, w_out, w_up, w_down, gains, biases, up_bias, image_cut, group_live, cotangent
+):
+    width = tokens.shape[1]
+    half = width // 2
+    part = width // COUNT
+    core = lax.axis_index("dp") % 2
+    me = (lax.axis_index("dp") * 2 + lax.axis_index("seq")).astype(jnp.int32)
+    swap = [(i, (i & ~3) | ((i & 1) << 1) | ((i >> 1) & 1)) for i in range(COUNT)]
+
+    def trade(value):
+        return lax.ppermute(value, BOTH, swap)
+
+    def across(value):
+        return hop(value, CORE, COUNT)
+
+    bounds = trade(jnp.concatenate([image_cut, group_live]))
+    tok = trade(tokens)
+    tok_far = across(tok)
+    cot = trade(cotangent)
+    meta = jnp.concatenate([jnp.stack([me, core.astype(jnp.int32)]), bounds])
+    here = core.astype(jnp.int32).reshape(1)
+
+    n1, q, k, v = qkv_call(meta, tok, tok_far, w_qkv, gains, biases)
+    o_far, lse_far = attend_call(meta, 1 - here, q, k, v)
+    a_got = across(o_far)
+    o_own, lse_own = attend_call(meta, here, q, k, v)
+    (block, gres, gb, ga_own, ga_send, small, gub), up, down = mid_call(
+        meta, tok, cot, o_own, a_got, w_out, w_up, w_down, gains, biases, up_bias
+    )
+    ga_far = across(ga_send)
+    block_out = trade(block)
+    out = wout_call(meta, o_own, a_got, gb)
+    dq, dk, dv = attend_back_call(
+        meta, q, k, v, ga_own, ga_far, o_own, o_far, lse_own, lse_far, 0, half // PAIR
+    )
+    zero = jnp.zeros((width,), F32)
+    rows = jnp.stack([zero, small[0], zero, small[1], zero, zero, small[2], small[3]])
+    units = gub.reshape(COUNT, 4, part).transpose(0, 2, 1).reshape(width, 4)
+    early = jnp.concatenate([rows.T, units, jnp.zeros((width, SMALL - 12), F32)], axis=1)
+    dn_own, dn_send, qkv = qkv_back_call(meta, n1, dq, dk, dv, w_qkv, tok, tok_far, early)
+    dn_got = across(dn_send)
+    grad_tokens = trade(tail_call(tok, gres, dn_own, dn_got, gains))
+
+    downs = reduce_streams(down, COUNT)
+    grad_wdown = jnp.concatenate(downs, axis=0)
+    grad_wup = jnp.concatenate(reduce_streams(up, COUNT), axis=1)
+    grad_wout = jnp.concatenate(reduce_streams(out, COUNT), axis=1)
+    sums = jnp.concatenate(reduce_streams(qkv, COUNT), axis=2)
+    kept, got = sums[0], across(sums[1])
+    first = jnp.where(core == 0, kept, got)
+    second = jnp.where(core == 0, got, kept)
+    cols = []
+    for i in range(3):
+        cols += [first[:, i * half : (i + 1) * half], second[:, i * half : (i + 1) * half]]
+    grad_qkv = jnp.concatenate(cols, axis=1)
+    little = kept[:, 3 * half :] + got[:, 3 * half :]
+    grad_gains = little[:, 0:2].T
+    grad_biases = little[:, 2:8].T
+    grad_upbias = little[:, 8:12].T.reshape(-1)
+    return (
+        block_out, grad_tokens, grad_qkv, grad_wout, grad_wup, grad_wdown, grad_gains, grad_biases, grad_upbias,
+    )
 
 
 def norm_rows(values, gain, shift):
@@ -185,4 +888,5 @@
         P(None, ("dp", "seq")),
         P(("dp", "seq")),
     )
-    return jax.shard_map(shards, mesh=mesh, in_specs=in_specs, out_specs=out_specs, check_vma=False)
+    fits = mesh.shape["seq"] == 2 and mesh.shape["dp"] * 2 == COUNT
+    return jax.shard_map(paired if fits else shards, mesh=mesh, in_specs=in_specs, out_specs=out_specs, check_vma=False)

time: 889 us -> 390 us (0.44)
  waiting for transfers between devices: 503 us -> 148 us
  matrix products: 245 us -> 0 us
  Pallas kernels: 0 us -> 119 us
  starting transfers between devices: 0.67 us -> 84.8 us
  blocking collectives: 41.1 us -> 0 us
  local copies, waits for them, and re-layouts: 40.6 us -> 11.2 us
  other arithmetic: 36.5 us -> 17.2 us
  between operations: 16.2 us -> 2.96 us
    reduce_scatter x5 -> x0, waiting for transfers between devices: 462 us -> none  [the longest x1 142 us: shards(): lax.psum_scatter(grad_wup, ('dp', 'seq'), scatter_dimension=0, tiled=True)]
    dot_general x96 -> x0, matrix products: 245 us -> none  [the longest x24 41.9 us: head_probs(): jnp.einsum('qd,kd->qk', query_head, key_head, preferred_element_type=jnp....]
    ppermute x0 -> x67, waiting for transfers between devices: none -> 148 us  [the longest x62 148 us: hop(): return lax.ppermute(value, BOTH, [(i, i ^ mask) for i in range(count)])]
    pallas_call x0 -> x8, Pallas kernels: none -> 119 us  [the longest x1 38.2 us: mid_call(): pl.pallas_call(mid_kernel, grid_spec=pltpu.PrefetchScalarGridSpec(num_sca...]
    ppermute x0 -> x67, starting transfers between devices: none -> 84.8 us  [the longest x62 77 us: hop(): return lax.ppermute(value, BOTH, [(i, i ^ mask) for i in range(count)])]
    unnamed x1 -> x0, blocking collectives: 41.1 us -> none
    all_gather x1 -> x0, waiting for transfers between devices: 40.3 us -> none  [shards(): kv_whole = lax.all_gather(kv_local, 'seq', axis=0, tiled=True)]
    reduce_sum x33 -> x0, other arithmetic: 21.3 us -> none  [the longest x24 12.4 us: head_probs(): return jax.nn.softmax(raw * 0.125 + mask, axis=-1)]
  transfers between devices with their start and end apart: 6 -> 67, of which waited for: 6 -> 39; matrix products, arithmetic and copies ran while one was open for 7% -> 6% of each run, Pallas kernels for 0% -> 20%
where the time goes in v1:
time: 390 us; the launch traced here: 383 us
  waiting for transfers between devices  148 us (38%)
  Pallas kernels  119 us (31%)
  starting transfers between devices  84.8 us (22%)
  other arithmetic  17.2 us (4%)
  local copies, waits for them, and re-layouts  11.2 us (3%)
    ppermute x62, waiting for transfers between devices, hop(): return lax.ppermute(value, BOTH, [(i, i ^ mask) for i in range(count)])  148 us
    ppermute x62, starting transfers between devices, hop(): return lax.ppermute(value, BOTH, [(i, i ^ mask) for i in range(count)])  77 us
    pallas_call x1, Pallas kernels, mid_call(): pl.pallas_call(mid_kernel, grid_spec=pltpu.PrefetchScalarGridSpec(num_sca...  38.2 us
    pallas_call x2, Pallas kernels, attend_call(): pl.pallas_call(attend_kernel, grid_spec=pltpu.PrefetchScalarGridSpec(num_...  28 us
    pallas_call x1, Pallas kernels, attend_back_call(): pl.pallas_call(attend_back_kernel, grid_spec=pltpu.PrefetchScalarGridSpec...  23.9 us
    pallas_call x1, Pallas kernels, qkv_back_call(): pl.pallas_call(qkv_back_kernel, grid_spec=pltpu.PrefetchScalarGridSpec(nu...  12.4 us
    convert_element_type x33, other arithmetic, reduce_streams(): keep = add_up(keep[0], arrived[0]).astype(BF16)  11.6 us
  transfers between devices with their start and end apart: 67, of which 39 were waited for; matrix products, arithmetic and copies ran while one was open for 6% of the time, Pallas kernels for 20%

profile of v1, /device:TPU:0, one launch (start us, length us, event | category | flops | bytes accessed | tf_op | source)
XLA Modules:
  0.0 383.3 jit_solution(5072616410879354256)
XLA Ops:
  2.4 13.1 %collective-permute-start.3 = (bf16[512,768]{1,0:T(8,128)(2,1)S(1)}, bf16[512,768]{1,0:T(8,128)(2,1)S(1)}, u32[]{:S(2)}, u32[]{:S(2)}) collective-permute-start(bf16[512,768]{1,0:T(8,128)(2,1)S(1)} %collective-permute-done.1.mine.tok.tok_mine), channel_id=1, source_target_pairs={{0,2},{1,3},{2,0},{3,1},{4,6},{5,7},{6,4},{7,5},{8,10},{9,11},{10,... | collective-permute-start | bytes 2359304 | tf_op jit(solution)/shard_map/ppermute | solution.py:49
  20.9 7.5 %qkv.1 = (bf16[1024,768]{1,0:T(8,128)(2,1)}, bf16[1024,384]{1,0:T(8,128)(2,1)}, bf16[1024,384]{1,0:T(8,128)(2,1)}, bf16[1024,384]{1,0:T(8,128)(2,1)}) custom-call(s32[4]{0:T(128)} %pad_add_fusion.1.meta, bf16[512,768]{1,0:T(8,128)(2,1)} %copy-done, bf16[512,768]{1,0:T(8,128)(2,1)} %copy-done.1, bf16[768,2304]{1,0:T(8,128)(2,1)} %wv.3, bf16[768,2304]{1,0:T(8,128)(2,1)} %wv.3, ...), custom_call_target="tpu_custom_call" | custom-call | tf_op jit(solution)/shard_map/qkv/pallas_call | solution.py:113
  28.4 13.3 %attend.3 = (bf16[512,384]{1,0:T(8,128)(2,1)}, f32[3,2,512]{2,1,0:T(2,128)}) custom-call(s32[4]{0:T(128)} %pad_add_fusion.1.meta, s32[1]{0:T(128)S(6)} %sub.3.which, bf16[1024,384]{1,0:T(8,128)(2,1)} %get-tuple-element.53.q_ref, bf16[1024,384]{1,0:T(8,128)(2,1)} %get-tuple-element.54.k_ref, bf16[1024,384]{1,0:T(8,128)(2,1)} %get-tuple-element.55.v_ref), custom_call_target="tpu_custom_call" | custom-call | tf_op jit(solution)/shard_map/attend/pallas_call | solution.py:225
  41.7 11.1 %collective-permute-start.4 = (bf16[512,384]{1,0:T(8,128)(2,1)}, bf16[512,384]{1,0:T(8,128)(2,1)S(1)}, u32[]{:S(2)}, u32[]{:S(2)}) collective-permute-start(bf16[512,384]{1,0:T(8,128)(2,1)} %get-tuple-element.57.o_other), channel_id=1, source_target_pairs={{0,2},{1,3},{2,0},{3,1},{4,6},{5,7},{6,4},{7,5},{8,10},{9,11},{10,... | collective-permute-start | bytes 1179656 | tf_op jit(solution)/shard_map/ppermute | solution.py:49
  52.8 14.8 %attend.2 = (bf16[512,384]{1,0:T(8,128)(2,1)}, f32[3,2,512]{2,1,0:T(2,128)}) custom-call(s32[4]{0:T(128)} %pad_add_fusion.1.meta, s32[1]{0:T(128)} %bitcast.1.which, bf16[1024,384]{1,0:T(8,128)(2,1)} %get-tuple-element.53.q_ref, bf16[1024,384]{1,0:T(8,128)(2,1)} %get-tuple-element.54.k_ref, bf16[1024,384]{1,0:T(8,128)(2,1)} %get-tuple-element.55.v_ref), custom_call_target="tpu_custom_call" | custom-call | tf_op jit(solution)/shard_map/attend/pallas_call | solution.py:225
  68.6 38.2 %mid.1 = (bf16[512,768]{1,0:T(8,128)(2,1)}, f32[512,768]{1,0:T(8,128)}, bf16[512,768]{1,0:T(8,128)(2,1)}, bf16[512,384]{1,0:T(8,128)(2,1)}, bf16[512,384]{1,0:T(...) custom-call(s32[4]{0:T(128)} %pad_add_fusion.1.meta, ...), custom_call_target="tpu_custom_call" | custom-call | tf_op jit(solution)/shard_map/mid/pallas_call | solution.py:494
  106.9 4.0 %wout.1 = (bf16[2,2,2,2,24,128]{5,4,3,2,1,0:T(8,128)(2,1)}, bf16[2,2,2,2,24,128]{5,4,3,2,1,0:T(8,128)(2,1)}, bf16[2,2,2,2,24,384]{5,4,3,2,1,0:T(8,128)(2,1)}, bf...) custom-call(s32[4]{0:T(128)} %pad_add_fusion.1.meta, ...), custom_call_target="tpu_custom_call" | custom-call | tf_op jit(solution)/shard_map/wout/pallas_call | solution.py:539
  117.8 4.1 %collective-permute-start.24 = (bf16[2,2,24,128]{3,2,1,0:T(8,128)(2,1)S(1)}, bf16[2,2,24,128]{3,2,1,0:T(8,128)(2,1)S(1)}, u32[]{:S(2)}, u32[]{:S(2)}) collective-permute-start(bf16[2,2,24,128]{3,2,1,0:T(8,128)(2,1)S(1)} %get-tuple-element.189), channel_id=1, source_target_pairs={{0,24},{1,25},{2,26},{3,27},{4,28},{5,29},{6,30},{7,31},{8,16},{9,... | collective-permute-start | bytes 73736 | tf_op jit(solution)/shard_map/ppermute | solution.py:49
  135.2 4.3 %collective-permute-done.33 = bf16[2,2,2,24,256]{4,3,2,1,0:T(8,128)(2,1)S(1)} collective-permute-done((bf16[2,2,2,24,256]{4,3,2,1,0:T(8,128)(2,1)S(1)}, bf16[2,2,2,24,256]{4,3,2,1,0:T(8,128)(2,1)S(1)}, u32[]{:S(2)}, u32[]{:S(2)}) %collective-permute-start.33) | collective-permute-done | bytes 98336 | tf_op jit(solution)/shard_map/ppermute | solution.py:49
  140.8 8.5 %collective-permute-done.28 = bf16[2,2,2,24,384]{4,3,2,1,0:T(8,128)(2,1)S(1)} collective-permute-done((bf16[2,2,2,24,384]{4,3,2,1,0:T(8,128)(2,1)S(1)}, bf16[2,2,2,24,384]{4,3,2,1,0:T(8,128)(2,1)S(1)}, u32[]{:S(2)}, u32[]{:S(2)}) %collective-permute-start.28) | collective-permute-done | bytes 147488 | tf_op jit(solution)/shard_map/ppermute | solution.py:49
  149.3 4.0 %collective-permute-done.34 = bf16[2,2,24,256]{3,2,1,0:T(8,128)(2,1)S(1)} collective-permute-done((bf16[2,2,24,256]{3,2,1,0:T(8,128)(2,1)S(1)}, bf16[2,2,24,256]{3,2,1,0:T(8,128)(2,1)S(1)}, u32[]{:S(2)}, u32[]{:S(2)}) %collective-permute-start.34) | collective-permute-done | bytes 49184 | tf_op jit(solution)/shard_map/ppermute | solution.py:49
  157.8 3.8 collective-permute-done.35
  161.6 3.9 %collective-permute-done.30 = bf16[2,24,384]{2,1,0:T(8,128)(2,1)S(1)} collective-permute-done((bf16[2,24,384]{2,1,0:T(8,128)(2,1)S(1)}, bf16[2,24,384]{2,1,0:T(8,128)(2,1)S(1)}, u32[]{:S(2)}, u32[]{:S(2)}) %collective-permute-start.30) | collective-permute-done | bytes 36896 | tf_op jit(solution)/shard_map/ppermute | solution.py:49
  165.5 3.6 collective-permute-start.36
  175.4 23.9 %attend_back.1 = (bf16[1024,384]{1,0:T(8,128)(2,1)}, bf16[1024,384]{1,0:T(8,128)(2,1)}, bf16[1024,384]{1,0:T(8,128)(2,1)}) custom-call(s32[4]{0:T(128)} %pad_add_fusion.1.meta, bf16[1024,384]{1,0:T(8,128)(2,1)} %get-tuple-element.53.q_ref, bf16[1024,384]{1,0:T(8,128)(2,1)} %get-tuple-element.54.k_ref, bf16[1024,384]{1,0:T(8,128)(2,1)} %get-tuple-element.55.v_ref, ...), custom_call_target="tpu_custom_call" | custom-call | tf_op jit(solution)/shard_map/attend_back/pallas_call | solution.py:315
  199.3 12.4 %qkv_back.1 = (f32[512,768]{1,0:T(8,128)}, bf16[512,768]{1,0:T(8,128)(2,1)}, bf16[2,2,2,2,24,384]{5,4,3,2,1,0:T(8,128)(2,1)}, bf16[2,2,2,2,24,384]{5,4,3,2,1,0:T...) custom-call(s32[4]{0:T(128)} %pad_add_fusion.1.meta, ...), custom_call_target="tpu_custom_call" | custom-call | tf_op jit(solution)/shard_map/qkv_back/pallas_call | solution.py:609
  215.6 6.5 %collective-permute-done.9 = bf16[2,2,2,2,24,384]{5,4,3,2,1,0:T(8,128)(2,1)S(1)} collective-permute-done((bf16[2,2,2,2,24,384]{5,4,3,2,1,0:T(8,128)(2,1)}, bf16[2,2,2,2,24,384]{5,4,3,2,1,0:T(8,128)(2,1)S(1)}, u32[]{:S(2)}, u32[]{:S(2)}) %collective-permute-start.9) | collective-permute-done | bytes 294944 | tf_op jit(solution)/shard_map/ppermute | solution.py:49
  224.8 9.2 %collective-permute-done.17 = bf16[2,2,2,2,24,512]{5,4,3,2,1,0:T(8,128)(2,1)S(1)} collective-permute-done((bf16[2,2,2,2,24,512]{5,4,3,2,1,0:T(8,128)(2,1)S(1)}, bf16[2,2,2,2,24,512]{5,4,3,2,1,0:T(8,128)(2,1)S(1)}, u32[]{:S(2)}, u32[]{:S(2)}) %collective-permute-start.17) | collective-permute-done | bytes 393248 | tf_op jit(solution)/shard_map/ppermute | solution.py:49
  240.7 4.6 %collective-permute-done.14 = bf16[2,2,2,24,384]{4,3,2,1,0:T(8,128)(2,1)S(1)} collective-permute-done((bf16[2,2,2,24,384]{4,3,2,1,0:T(8,128)(2,1)S(1)}, bf16[2,2,2,24,384]{4,3,2,1,0:T(8,128)(2,1)S(1)}, u32[]{:S(2)}, u32[]{:S(2)}) %collective-permute-start.14) | collective-permute-done | bytes 147488 | tf_op jit(solution)/shard_map/ppermute | solution.py:49
  250.5 4.9 %collective-permute-done.38 = bf16[2,2,2,24,768]{4,3,2,1,0:T(8,128)(2,1)S(1)} collective-permute-done((bf16[2,2,2,24,768]{4,3,2,1,0:T(8,128)(2,1)S(1)}, bf16[2,2,2,24,768]{4,3,2,1,0:T(8,128)(2,1)S(1)}, u32[]{:S(2)}, u32[]{:S(2)}) %collective-permute-start.38) | collective-permute-done | bytes 294944 | tf_op jit(solution)/shard_map/ppermute | solution.py:49
  257.7 5.8 %collective-permute-done.53 = bf16[2,2,2,24,768]{4,3,2,1,0:T(8,128)(2,1)S(1)} collective-permute-done((bf16[2,2,2,24,768]{4,3,2,1,0:T(8,128)(2,1)S(1)}, bf16[2,2,2,24,768]{4,3,2,1,0:T(8,128)(2,1)S(1)}, u32[]{:S(2)}, u32[]{:S(2)}) %collective-permute-start.53) | collective-permute-done | bytes 294944 | tf_op jit(solution)/shard_map/ppermute | solution.py:49
  263.7 4.3 %collective-permute-done.11 = bf16[2,2,24,384]{3,2,1,0:T(8,128)(2,1)S(1)} collective-permute-done((bf16[2,2,24,384]{3,2,1,0:T(8,128)(2,1)S(1)}, bf16[2,2,24,384]{3,2,1,0:T(8,128)(2,1)S(1)}, u32[]{:S(2)}, u32[]{:S(2)}) %collective-permute-start.11) | collective-permute-done | bytes 73760 | tf_op jit(solution)/shard_map/ppermute | solution.py:49
  267.9 4.3 %collective-permute-done.15 = bf16[2,2,24,384]{3,2,1,0:T(8,128)(2,1)S(1)} collective-permute-done((bf16[2,2,24,384]{3,2,1,0:T(8,128)(2,1)S(1)}, bf16[2,2,24,384]{3,2,1,0:T(8,128)(2,1)S(1)}, u32[]{:S(2)}, u32[]{:S(2)}) %collective-permute-start.15) | collective-permute-done | bytes 73760 | tf_op jit(solution)/shard_map/ppermute | solution.py:49
  272.3 5.8 %collective-permute-done.12 = bf16[2,24,384]{2,1,0:T(8,128)(2,1)S(1)} collective-permute-done((bf16[2,24,384]{2,1,0:T(8,128)(2,1)S(1)}, bf16[2,24,384]{2,1,0:T(8,128)(2,1)S(1)}, u32[]{:S(2)}, u32[]{:S(2)}) %collective-permute-start.12) | collective-permute-done | bytes 36896 | tf_op jit(solution)/shard_map/ppermute | solution.py:49
  278.2 5.8 %collective-permute-done.16 = bf16[2,24,384]{2,1,0:T(8,128)(2,1)S(1)} collective-permute-done((bf16[2,24,384]{2,1,0:T(8,128)(2,1)S(1)}, bf16[2,24,384]{2,1,0:T(8,128)(2,1)S(1)}, u32[]{:S(2)}, u32[]{:S(2)}) %collective-permute-start.16) | collective-permute-done | bytes 36896 | tf_op jit(solution)/shard_map/ppermute | solution.py:49
  293.9 6.6 %collective-permute-done.19 = bf16[2,2,24,512]{3,2,1,0:T(8,128)(2,1)S(1)} collective-permute-done((bf16[2,2,24,512]{3,2,1,0:T(8,128)(2,1)S(1)}, bf16[2,2,24,512]{3,2,1,0:T(8,128)(2,1)S(1)}, u32[]{:S(2)}, u32[]{:S(2)}) %collective-permute-start.19) | collective-permute-done | bytes 98336 | tf_op jit(solution)/shard_map/ppermute | solution.py:49
  300.6 4.1 %collective-permute-done.40 = bf16[2,24,768]{2,1,0:T(8,128)(2,1)S(1)} collective-permute-done((bf16[2,24,768]{2,1,0:T(8,128)(2,1)S(1)}, bf16[2,24,768]{2,1,0:T(8,128)(2,1)S(1)}, u32[]{:S(2)}, u32[]{:S(2)}) %collective-permute-start.40) | collective-permute-done | bytes 73760 | tf_op jit(solution)/shard_map/ppermute | solution.py:49
  305.0 4.3 %collective-permute-done.55 = bf16[2,24,768]{2,1,0:T(8,128)(2,1)S(1)} collective-permute-done((bf16[2,24,768]{2,1,0:T(8,128)(2,1)S(1)}, bf16[2,24,768]{2,1,0:T(8,128)(2,1)S(1)}, u32[]{:S(2)}, u32[]{:S(2)}) %collective-permute-start.55) | collective-permute-done | bytes 73760 | tf_op jit(solution)/shard_map/ppermute | solution.py:49
  309.3 4.6 %collective-permute-done.20 = bf16[2,24,512]{2,1,0:T(8,128)(2,1)S(1)} collective-permute-done((bf16[2,24,512]{2,1,0:T(8,128)(2,1)S(1)}, bf16[2,24,512]{2,1,0:T(8,128)(2,1)S(1)}, u32[]{:S(2)}, u32[]{:S(2)}) %collective-permute-start.20) | collective-permute-done | bytes 49184 | tf_op jit(solution)/shard_map/ppermute | solution.py:49
  322.8 4.7 %tail.1 = bf16[512,768]{1,0:T(8,128)(2,1)} custom-call(bf16[512,768]{1,0:T(8,128)(2,1)} %copy-done, f32[512,768]{1,0:T(8,128)} %get-tuple-element.59.gres, f32[512,768]{1,0:T(8,128)} %get-tuple-element.70.dn_own, bf16[512,768]{1,0:T(8,128)(2,1)} %copy-done.8, f32[2,768]{1,0:T(2,128)} %gains.5), custom_call_target="tpu_custom_call" | custom-call | tf_op jit(solution)/shard_map/tail/pallas_call | solution.py:641
  340.4 5.4 %collective-permute-done.64 = bf16[2,2,32,768]{3,2,1,0:T(8,128)(2,1)} collective-permute-done((bf16[2,2,32,768]{3,2,1,0:T(8,128)(2,1)}, bf16[2,2,32,768]{3,2,1,0:T(8,128)(2,1)}, u32[]{:S(2)}, u32[]{:S(2)}) %collective-permute-start.64) | collective-permute-done | bytes 196640 | tf_op jit(solution)/shard_map/ppermute | solution.py:49
  375.8 4.8 %collective-permute-done.61 = bf16[40,768]{1,0:T(8,128)(2,1)S(1)} collective-permute-done((bf16[40,768]{1,0:T(8,128)(2,1)S(1)}, bf16[40,768]{1,0:T(8,128)(2,1)S(1)}, u32[]{:S(2)}, u32[]{:S(2)}) %collective-permute-start.61) | collective-permute-done | bytes 61472 | tf_op jit(solution)/shard_map/ppermute | solution.py:49
  (266 shorter events, 124.0 us)
Async XLA Ops:
  2.4 17.5 %collective-permute-start.3 = (bf16[512,768]{1,0:T(8,128)(2,1)S(1)}, bf16[512,768]{1,0:T(8,128)(2,1)S(1)}, u32[]{:S(2)}, u32[]{:S(2)}) collective-permute-start(bf16[512,768]{1,0:T(8,128)(2,1)S(1)} %collective-permute-done.1.mine.tok.tok_mine), channel_id=1, source_target_pairs={{0,2},{1,3},{2,0},{3,1},{4,6},{5,7},{6,4},{7,5},{8,10},{9,11},{10,... | collective-permute-start | bytes 2359304 | tf_op jit(solution)/shard_map/ppermute | solution.py:49
  15.5 52.1 %collective-permute-start.2 = (bf16[512,768]{1,0:T(8,128)(2,1)}, bf16[512,768]{1,0:T(8,128)(2,1)S(1)}, u32[]{:S(2)}, u32[]{:S(2)}) collective-permute-start(bf16[512,768]{1,0:T(8,128)(2,1)} %param.21), channel_id=1, source_target_pairs={{0,0},{1,2},{2,1},{3,3},{4,4},{5,6},{6,5},{7,7},{8,8},{9,10},{10,9... | collective-permute-start | bytes 2359304 | tf_op jit(solution)/shard_map/ppermute | solution.py:663
  41.7 25.9 %collective-permute-start.4 = (bf16[512,384]{1,0:T(8,128)(2,1)}, bf16[512,384]{1,0:T(8,128)(2,1)S(1)}, u32[]{:S(2)}, u32[]{:S(2)}) collective-permute-start(bf16[512,384]{1,0:T(8,128)(2,1)} %get-tuple-element.57.o_other), channel_id=1, source_target_pairs={{0,2},{1,3},{2,0},{3,1},{4,6},{5,7},{6,4},{7,5},{8,10},{9,11},{10,... | collective-permute-start | bytes 1179656 | tf_op jit(solution)/shard_map/ppermute | solution.py:49
  127.1 47.5 %collective-permute-start.6 = (bf16[512,384]{1,0:T(8,128)(2,1)S(1)}, bf16[512,384]{1,0:T(8,128)(2,1)S(1)}, u32[]{:S(2)}, u32[]{:S(2)}) collective-permute-start(bf16[512,384]{1,0:T(8,128)(2,1)S(1)} %copy-done.26), channel_id=1, source_target_pairs={{0,2},{1,3},{2,0},{3,1},{4,6},{5,7},{6,4},{7,5},{8,10},{9,11},{10,... | collective-permute-start | bytes 1179656 | tf_op jit(solution)/shard_map/ppermute | solution.py:49
  127.8 84.7 %collective-permute-start.37 = (bf16[2,2,2,2,24,768]{5,4,3,2,1,0:T(8,128)(2,1)}, bf16[2,2,2,2,24,768]{5,4,3,2,1,0:T(8,128)(2,1)S(1)}, u32[]{:S(2)}, u32[]{:S(2)}) collective-permute-start(bf16[2,2,2,2,24,768]{5,4,3,2,1,0:T(8,128)(2,1)} %get-tuple-element.86), channel_id=1, source_target_pairs={{0,2},{1,3},{2,0},{3,1},{4,6},{5,7},{6,4},{7,5},{8,10},{9,11},{10,... | collective-permute-start | bytes 1769480 | tf_op jit(solution)/shard_map/ppermute | solution.py:49
  131.9 80.9 %collective-permute-start.52 = (bf16[2,2,2,2,24,768]{5,4,3,2,1,0:T(8,128)(2,1)}, bf16[2,2,2,2,24,768]{5,4,3,2,1,0:T(8,128)(2,1)S(1)}, u32[]{:S(2)}, u32[]{:S(2)}) collective-permute-start(bf16[2,2,2,2,24,768]{5,4,3,2,1,0:T(8,128)(2,1)} %get-tuple-element.92), channel_id=1, source_target_pairs={{0,2},{1,3},{2,0},{3,1},{4,6},{5,7},{6,4},{7,5},{8,10},{9,11},{10,... | collective-permute-start | bytes 1769480 | tf_op jit(solution)/shard_map/ppermute | solution.py:49
  131.9 91.3 %collective-permute-start.5 = (bf16[512,768]{1,0:T(8,128)(2,1)}, bf16[512,768]{1,0:T(8,128)(2,1)S(1)}, u32[]{:S(2)}, u32[]{:S(2)}) collective-permute-start(bf16[512,768]{1,0:T(8,128)(2,1)} %get-tuple-element.58), channel_id=1, source_target_pairs={{0,0},{1,2},{2,1},{3,3},{4,4},{5,6},{6,5},{7,7},{8,8},{9,10},{10,9... | collective-permute-start | bytes 2359304 | tf_op jit(solution)/shard_map/ppermute | solution.py:663
  139.5 9.8 %collective-permute-start.28 = (bf16[2,2,2,24,384]{4,3,2,1,0:T(8,128)(2,1)S(1)}, bf16[2,2,2,24,384]{4,3,2,1,0:T(8,128)(2,1)S(1)}, u32[]{:S(2)}, u32[]{:S(2)}) collective-permute-start(bf16[2,2,2,24,384]{4,3,2,1,0:T(8,128)(2,1)S(1)} %get-tuple-element.151), channel_id=1, source_target_pairs={{0,1},{1,0},{2,3},{3,2},{4,5},{5,4},{6,7},{7,6},{8,9},{9,8},{10,11... | collective-permute-start | bytes 442376 | tf_op jit(solution)/shard_map/ppermute | solution.py:49
  171.0 40.7 %collective-permute-start.31 = (bf16[24,384]{1,0:T(8,128)(2,1)S(1)}, bf16[24,384]{1,0:T(8,128)(2,1)S(1)}, u32[]{:S(2)}, u32[]{:S(2)}) collective-permute-start(bf16[24,384]{1,0:T(8,128)(2,1)S(1)} %fusion.115), channel_id=1, source_target_pairs={{0,24},{1,25},{2,26},{3,27},{4,28},{5,29},{6,30},{7,31},{8,16},{9,... | collective-permute-start | bytes 55304 | tf_op jit(solution)/shard_map/ppermute | solution.py:49
  174.7 48.6 %collective-permute-start.62 = (bf16[2,2,2,2,32,768]{5,4,3,2,1,0:T(8,128)(2,1)S(1)}, bf16[2,2,2,2,32,768]{5,4,3,2,1,0:T(8,128)(2,1)S(1)}, u32[]{:S(2)}, u32[]{:S(2)}) collective-permute-start(bf16[2,2,2,2,32,768]{5,4,3,2,1,0:T(8,128)(2,1)S(1)} %copy-done.24), channel_id=1, source_target_pairs={{0,2},{1,3},{2,0},{3,1},{4,6},{5,7},{6,4},{7,5},{8,10},{9,11},{10,... | collective-permute-start | bytes 2359304 | tf_op jit(solution)/shard_map/ppermute | solution.py:49
  211.7 34.1 %collective-permute-start.42 = (bf16[2,2,2,2,24,1152]{5,4,3,2,1,0:T(8,128)(2,1)S(1)}, bf16[2,2,2,2,24,1152]{5,4,3,2,1,0:T(8,128)(2,1)S(1)}, u32[]{:S(2)}, u32[]{:S(2)}) collective-permute-start(bf16[2,2,2,2,24,1152]{5,4,3,2,1,0:T(8,128)(2,1)S(1)} %copy-done.23), channel_id=1, source_target_pairs={{0,2},{1,3},{2,0},{3,1},{4,6},{5,7},{6,4},{7,5},{8,10},{9,11},{10,... | collective-permute-start | bytes 2654216 | tf_op jit(solution)/shard_map/ppermute | solution.py:49
  212.5 9.6 %collective-permute-start.9 = (bf16[2,2,2,2,24,384]{5,4,3,2,1,0:T(8,128)(2,1)}, bf16[2,2,2,2,24,384]{5,4,3,2,1,0:T(8,128)(2,1)S(1)}, u32[]{:S(2)}, u32[]{:S(2)}) collective-permute-start(bf16[2,2,2,2,24,384]{5,4,3,2,1,0:T(8,128)(2,1)} %get-tuple-element.73), channel_id=1, source_target_pairs={{0,1},{1,0},{2,3},{3,2},{4,5},{5,4},{6,7},{7,6},{8,9},{9,8},{10,11... | collective-permute-start | bytes 884744 | tf_op jit(solution)/shard_map/ppermute | solution.py:49
  212.8 10.3 %collective-permute-start.13 = (bf16[2,2,2,2,24,384]{5,4,3,2,1,0:T(8,128)(2,1)S(1)}, bf16[2,2,2,2,24,384]{5,4,3,2,1,0:T(8,128)(2,1)S(1)}, u32[]{:S(2)}, u32[]{:S(2)}) collective-permute-start(bf16[2,2,2,2,24,384]{5,4,3,2,1,0:T(8,128)(2,1)S(1)} %copy-done.29), channel_id=1, source_target_pairs={{0,4},{1,5},{2,6},{3,7},{4,0},{5,1},{6,2},{7,3},{8,12},{9,13},{10,... | collective-permute-start | bytes 884744 | tf_op jit(solution)/shard_map/ppermute | solution.py:49
  222.1 26.3 %collective-permute-start.47 = (bf16[2,2,2,2,24,1152]{5,4,3,2,1,0:T(8,128)(2,1)S(1)}, bf16[2,2,2,2,24,1152]{5,4,3,2,1,0:T(8,128)(2,1)S(1)}, u32[]{:S(2)}, u32[]{:S(2)}) collective-permute-start(bf16[2,2,2,2,24,1152]{5,4,3,2,1,0:T(8,128)(2,1)S(1)} %copy-done.22), channel_id=1, source_target_pairs={{0,2},{1,3},{2,0},{3,1},{4,6},{5,7},{6,4},{7,5},{8,10},{9,11},{10,... | collective-permute-start | bytes 2654216 | tf_op jit(solution)/shard_map/ppermute | solution.py:49
  223.1 10.9 %collective-permute-start.17 = (bf16[2,2,2,2,24,512]{5,4,3,2,1,0:T(8,128)(2,1)S(1)}, bf16[2,2,2,2,24,512]{5,4,3,2,1,0:T(8,128)(2,1)S(1)}, u32[]{:S(2)}, u32[]{:S(2)}) collective-permute-start(bf16[2,2,2,2,24,512]{5,4,3,2,1,0:T(8,128)(2,1)S(1)} %copy-done.27), channel_id=1, source_target_pairs={{0,8},{1,9},{2,10},{3,11},{4,12},{5,13},{6,14},{7,15},{8,0},{9,1},... | collective-permute-start | bytes 1179656 | tf_op jit(solution)/shard_map/ppermute | solution.py:49
  223.2 61.1 %collective-permute-start.57 = (bf16[2,2,2,2,40,768]{5,4,3,2,1,0:T(8,128)(2,1)S(1)}, bf16[2,2,2,2,40,768]{5,4,3,2,1,0:T(8,128)(2,1)S(1)}, u32[]{:S(2)}, u32[]{:S(2)}) collective-permute-start(bf16[2,2,2,2,40,768]{5,4,3,2,1,0:T(8,128)(2,1)S(1)} %copy-done.21), channel_id=1, source_target_pairs={{0,2},{1,3},{2,0},{3,1},{4,6},{5,7},{6,4},{7,5},{8,10},{9,11},{10,... | collective-permute-start | bytes 2949128 | tf_op jit(solution)/shard_map/ppermute | solution.py:49
  223.3 98.6 %collective-permute-start.7 = (bf16[512,768]{1,0:T(8,128)(2,1)S(1)}, bf16[512,768]{1,0:T(8,128)(2,1)S(1)}, u32[]{:S(2)}, u32[]{:S(2)}) collective-permute-start(bf16[512,768]{1,0:T(8,128)(2,1)S(1)} %copy-done.25), channel_id=1, source_target_pairs={{0,2},{1,3},{2,0},{3,1},{4,6},{5,7},{6,4},{7,5},{8,10},{9,11},{10,... | collective-permute-start | bytes 2359304 | tf_op jit(solution)/shard_map/ppermute | solution.py:49
  245.2 10.1 %collective-permute-start.38 = (bf16[2,2,2,24,768]{4,3,2,1,0:T(8,128)(2,1)S(1)}, bf16[2,2,2,24,768]{4,3,2,1,0:T(8,128)(2,1)S(1)}, u32[]{:S(2)}, u32[]{:S(2)}) collective-permute-start(bf16[2,2,2,24,768]{4,3,2,1,0:T(8,128)(2,1)S(1)} %get-tuple-element.135), channel_id=1, source_target_pairs={{0,8},{1,9},{2,10},{3,11},{4,12},{5,13},{6,14},{7,15},{8,0},{9,1},... | collective-permute-start | bytes 884744 | tf_op jit(solution)/shard_map/ppermute | solution.py:49
  245.9 17.7 %collective-permute-start.53 = (bf16[2,2,2,24,768]{4,3,2,1,0:T(8,128)(2,1)S(1)}, bf16[2,2,2,24,768]{4,3,2,1,0:T(8,128)(2,1)S(1)}, u32[]{:S(2)}, u32[]{:S(2)}) collective-permute-start(bf16[2,2,2,24,768]{4,3,2,1,0:T(8,128)(2,1)S(1)} %get-tuple-element.133), channel_id=1, source_target_pairs={{0,8},{1,9},{2,10},{3,11},{4,12},{5,13},{6,14},{7,15},{8,0},{9,1},... | collective-permute-start | bytes 884744 | tf_op jit(solution)/shard_map/ppermute | solution.py:49
  248.4 40.4 %collective-permute-start.18 = (bf16[2,2,2,24,512]{4,3,2,1,0:T(8,128)(2,1)S(1)}, bf16[2,2,2,24,512]{4,3,2,1,0:T(8,128)(2,1)S(1)}, u32[]{:S(2)}, u32[]{:S(2)}) collective-permute-start(bf16[2,2,2,24,512]{4,3,2,1,0:T(8,128)(2,1)S(1)} %get-tuple-element.145), channel_id=1, source_target_pairs={{0,24},{1,25},{2,26},{3,27},{4,28},{5,29},{6,30},{7,31},{8,16},{9,... | collective-permute-start | bytes 589832 | tf_op jit(solution)/shard_map/ppermute | solution.py:49
  255.4 72.1 %collective-permute-start.63 = (bf16[2,2,2,32,768]{4,3,2,1,0:T(8,128)(2,1)}, bf16[2,2,2,32,768]{4,3,2,1,0:T(8,128)(2,1)S(1)}, u32[]{:S(2)}, u32[]{:S(2)}) collective-permute-start(bf16[2,2,2,32,768]{4,3,2,1,0:T(8,128)(2,1)} %get-tuple-element.131), channel_id=1, source_target_pairs={{0,4},{1,5},{2,6},{3,7},{4,0},{5,1},{6,2},{7,3},{8,12},{9,13},{10,... | collective-permute-start | bytes 1179656 | tf_op jit(solution)/shard_map/ppermute | solution.py:49
  284.3 8.1 %collective-permute-start.54 = (bf16[2,2,24,768]{3,2,1,0:T(8,128)(2,1)S(1)}, bf16[2,2,24,768]{3,2,1,0:T(8,128)(2,1)S(1)}, u32[]{:S(2)}, u32[]{:S(2)}) collective-permute-start(bf16[2,2,24,768]{3,2,1,0:T(8,128)(2,1)S(1)} %get-tuple-element.147), channel_id=1, source_target_pairs={{0,24},{1,25},{2,26},{3,27},{4,28},{5,29},{6,30},{7,31},{8,16},{9,... | collective-permute-start | bytes 442376 | tf_op jit(solution)/shard_map/ppermute | solution.py:49
  288.9 49.0 %collective-permute-start.43 = (bf16[2,2,2,24,1152]{4,3,2,1,0:T(8,128)(2,1)}, bf16[2,2,2,24,1152]{4,3,2,1,0:T(8,128)(2,1)}, u32[]{:S(2)}, u32[]{:S(2)}) collective-permute-start(bf16[2,2,2,24,1152]{4,3,2,1,0:T(8,128)(2,1)} %get-tuple-element.127), channel_id=1, source_target_pairs={{0,1},{1,0},{2,3},{3,2},{4,5},{5,4},{6,7},{7,6},{8,9},{9,8},{10,11... | collective-permute-start | bytes 1327112 | tf_op jit(solution)/shard_map/ppermute | solution.py:49
  290.9 56.1 %collective-permute-start.48 = (bf16[2,2,2,24,1152]{4,3,2,1,0:T(8,128)(2,1)}, bf16[2,2,2,24,1152]{4,3,2,1,0:T(8,128)(2,1)}, u32[]{:S(2)}, u32[]{:S(2)}) collective-permute-start(bf16[2,2,2,24,1152]{4,3,2,1,0:T(8,128)(2,1)} %get-tuple-element.129), channel_id=1, source_target_pairs={{0,4},{1,5},{2,6},{3,7},{4,0},{5,1},{6,2},{7,3},{8,12},{9,13},{10,... | collective-permute-start | bytes 1327112 | tf_op jit(solution)/shard_map/ppermute | solution.py:49
  292.4 8.0 %collective-permute-start.19 = (bf16[2,2,24,512]{3,2,1,0:T(8,128)(2,1)S(1)}, bf16[2,2,24,512]{3,2,1,0:T(8,128)(2,1)S(1)}, u32[]{:S(2)}, u32[]{:S(2)}) collective-permute-start(bf16[2,2,24,512]{3,2,1,0:T(8,128)(2,1)S(1)} %get-tuple-element.167), channel_id=1, source_target_pairs={{0,4},{1,5},{2,6},{3,7},{4,0},{5,1},{6,2},{7,3},{8,12},{9,13},{10,... | collective-permute-start | bytes 294920 | tf_op jit(solution)/shard_map/ppermute | solution.py:49
  321.9 29.9 %collective-permute-start.58 = (bf16[2,2,2,40,768]{4,3,2,1,0:T(8,128)(2,1)}, bf16[2,2,2,40,768]{4,3,2,1,0:T(8,128)(2,1)}, u32[]{:S(2)}, u32[]{:S(2)}) collective-permute-start(bf16[2,2,2,40,768]{4,3,2,1,0:T(8,128)(2,1)} %get-tuple-element.125), channel_id=1, source_target_pairs={{0,1},{1,0},{2,3},{3,2},{4,5},{5,4},{6,7},{7,6},{8,9},{9,8},{10,11... | collective-permute-start | bytes 1474568 | tf_op jit(solution)/shard_map/ppermute | solution.py:49
  321.9 8.1 %collective-permute-start.21 = (f32[24,1280]{1,0:T(8,128)S(1)}, f32[24,1280]{1,0:T(8,128)S(1)}, u32[]{:S(2)}, u32[]{:S(2)}) collective-permute-start(f32[24,1280]{1,0:T(8,128)S(1)} %get-tuple-element.181), channel_id=1, source_target_pairs={{0,2},{1,3},{2,0},{3,1},{4,6},{5,7},{6,4},{7,5},{8,10},{9,11},{10,... | collective-permute-start | bytes 368648 | tf_op jit(solution)/shard_map/ppermute | solution.py:49
  327.4 53.9 %collective-permute-start.8 = (bf16[512,768]{1,0:T(8,128)(2,1)}, bf16[512,768]{1,0:T(8,128)(2,1)S(1)}, u32[]{:S(2)}, u32[]{:S(2)}) collective-permute-start(bf16[512,768]{1,0:T(8,128)(2,1)} %tail.1), channel_id=1, source_target_pairs={{0,0},{1,2},{2,1},{3,3},{4,4},{5,6},{6,5},{7,7},{8,8},{9,10},{10,9... | collective-permute-start | bytes 2359304 | tf_op jit(solution)/shard_map/ppermute | solution.py:663
  330.0 15.9 %collective-permute-start.64 = (bf16[2,2,32,768]{3,2,1,0:T(8,128)(2,1)}, bf16[2,2,32,768]{3,2,1,0:T(8,128)(2,1)}, u32[]{:S(2)}, u32[]{:S(2)}) collective-permute-start(bf16[2,2,32,768]{3,2,1,0:T(8,128)(2,1)} %get-tuple-element.143), channel_id=1, source_target_pairs={{0,1},{1,0},{2,3},{3,2},{4,5},{5,4},{6,7},{7,6},{8,9},{9,8},{10,11... | collective-permute-start | bytes 589832 | tf_op jit(solution)/shard_map/ppermute | solution.py:49
  339.1 18.9 %collective-permute-start.44 = (bf16[2,2,24,1152]{3,2,1,0:T(8,128)(2,1)S(1)}, bf16[2,2,24,1152]{3,2,1,0:T(8,128)(2,1)S(1)}, u32[]{:S(2)}, u32[]{:S(2)}) collective-permute-start(bf16[2,2,24,1152]{3,2,1,0:T(8,128)(2,1)S(1)} %get-tuple-element.139), channel_id=1, source_target_pairs={{0,4},{1,5},{2,6},{3,7},{4,0},{5,1},{6,2},{7,3},{8,12},{9,13},{10,... | collective-permute-start | bytes 663560 | tf_op jit(solution)/shard_map/ppermute | solution.py:49
  348.1 10.1 %collective-permute-start.49 = (bf16[2,2,24,1152]{3,2,1,0:T(8,128)(2,1)S(1)}, bf16[2,2,24,1152]{3,2,1,0:T(8,128)(2,1)S(1)}, u32[]{:S(2)}, u32[]{:S(2)}) collective-permute-start(bf16[2,2,24,1152]{3,2,1,0:T(8,128)(2,1)S(1)} %get-tuple-element.141), channel_id=1, source_target_pairs={{0,1},{1,0},{2,3},{3,2},{4,5},{5,4},{6,7},{7,6},{8,9},{9,8},{10,11... | collective-permute-start | bytes 663560 | tf_op jit(solution)/shard_map/ppermute | solution.py:49
  353.0 16.1 %collective-permute-start.59 = (bf16[2,2,40,768]{3,2,1,0:T(8,128)(2,1)S(1)}, bf16[2,2,40,768]{3,2,1,0:T(8,128)(2,1)S(1)}, u32[]{:S(2)}, u32[]{:S(2)}) collective-permute-start(bf16[2,2,40,768]{3,2,1,0:T(8,128)(2,1)S(1)} %get-tuple-element.137), channel_id=1, source_target_pairs={{0,4},{1,5},{2,6},{3,7},{4,0},{5,1},{6,2},{7,3},{8,12},{9,13},{10,... | collective-permute-start | bytes 737288 | tf_op jit(solution)/shard_map/ppermute | solution.py:49
  (66 other events, 553.0 us)
